TPU v7x, 32 devices: a whole 2x2x4 slice. The times are simulated.
32 devices in a mesh: ctx: 8 (over z, x), head: 4 (over y, core).
Axes of the slice: x: 2, y: 2, z: 4, core: 2. Of those that a mesh axis runs over, the one named last changes fastest.
Arguments:
- qkv: bfloat16 [4096, 12288], P(('ctx', 'head')), may hold values from -26 to 26
- grad_out: bfloat16 [4096, 4096], P(('ctx', 'head')), may hold values from -6 to 6
- key_lists: int32 [32, 4], P('ctx'), may hold values from 0 to 31, as said below
- live_counts: int32 [32], P('ctx'), may hold values from 1 to 4
Outputs:
- grad_qkv: bfloat16 [4096, 12288], P(('ctx', 'head'))
Inputs may be any that keep to these rules, and one draw needn't show every extreme that they name: `key_lists`: each entry names a block whose index of ctx is within 2 of its query block's and which is not within one block of its query block; the 4 entries of a row differ. Over all 4 entries of all rows (live or not) of one index of ctx, the blocks named on any other index of ctx are at most 2 of its blocks, and this is reached.
All inputs are finite; a program needn't handle non-finite values.
Results may differ from a plain program's by a relative error of at most 0.008.
Values may be sent and summed in bfloat16 or wider, within the bound.
A program may use at most 192 MiB of HBM per device.

v0:
```python
import jax
import jax.numpy as jnp
from jax import lax
from jax.sharding import PartitionSpec as P

HD = 128
BLK = 128
SEARCHER_TILES = 4
DRAWN_TARGET_SET = 4
SPAN = 2
NAMED_TILE_LIMIT = 2


def extended_2(cells, sides, width):
    for axis, dim in sides:
        count = lax.axis_size(axis)
        ends = count - 1
        head = lax.slice_in_dim(cells, 0, width, axis=dim)
        tail = lax.slice_in_dim(cells, cells.shape[dim] - width, cells.shape[dim], axis=dim)
        cells = jnp.concatenate(
            [
                lax.ppermute(tail, axis, [(i, (i + 1) % count) for i in range(ends)]),
                cells,
                lax.ppermute(head, axis, [((i + 1) % count, i) for i in range(ends)]),
            ],
            axis=dim,
        )
    return cells


def from_behind(value, axis, steps):
    count = lax.axis_size(axis)
    initial, last = (max(0, -steps), min(count, count - steps))
    return lax.ppermute(value, axis, [(source, source + steps) for source in range(initial, last)])


def block_grads(query_part, grad_part, key_part, value_part, usable):
    scaling = HD ** (-0.5)
    tile_merits = (
        jnp.einsum("qhd,nkhd->hqnk", query_part, key_part, preferred_element_type=jnp.float32)
        * scaling
    )
    weight = usable.astype(jnp.float32)[None, None, :, None]
    masked = jnp.where(weight > 0.0, tile_merits, -1e30)
    highest = jnp.max(masked, axis=(2, 3), keepdims=True)
    powers = jnp.exp(masked - highest) * weight
    soft_weights = powers / jnp.sum(powers, axis=(2, 3), keepdims=True)
    grad_soft = jnp.einsum(
        "qhd,nkhd->hqnk", grad_part, value_part, preferred_element_type=jnp.float32
    )
    row_delta = jnp.sum(soft_weights * grad_soft, axis=(2, 3), keepdims=True)
    grad_scores = soft_weights * (grad_soft - row_delta)
    soft_low = soft_weights.astype(jnp.bfloat16)
    scores_low = grad_scores.astype(jnp.bfloat16)
    grad_values = jnp.einsum(
        "hqnk,qhd->nkhd", soft_low, grad_part, preferred_element_type=jnp.float32
    )
    grad_keys = (
        jnp.einsum("hqnk,qhd->nkhd", scores_low, query_part, preferred_element_type=jnp.float32)
        * scaling
    )
    grad_query = (
        jnp.einsum("hqnk,nkhd->qhd", scores_low, key_part, preferred_element_type=jnp.float32)
        * scaling
    )
    return (grad_query, jnp.stack([grad_keys, grad_values], axis=3))


def needed_blocks(list_rows, owner_shard):
    targets = owner_shard * SEARCHER_TILES + jnp.arange(SEARCHER_TILES, dtype=jnp.int32)
    matches = list_rows[:, :, None] == targets[None, None, :]
    return jnp.any(matches, axis=(0, 1))


def slot_numbers(needed):
    block_order = jnp.arange(SEARCHER_TILES, dtype=jnp.int32)
    earlier = block_order[None, :] < block_order[:, None]
    return jnp.sum(jnp.where(earlier & needed[None, :], 1, 0), axis=1).astype(jnp.int32)


def select_table(needed):
    slot_of = slot_numbers(needed)
    slot_range = jnp.arange(NAMED_TILE_LIMIT, dtype=jnp.int32)
    return (needed[None, :] & (slot_of[None, :] == slot_range[:, None])).astype(jnp.float32)


def shards(qkv, grad_out, key_lists, live_counts):
    merged, grad_rows = (
        lax.all_to_all(qkv, "head", split_axis=1, concat_axis=0, tiled=True),
        lax.all_to_all(grad_out, "head", split_axis=1, concat_axis=0, tiled=True),
    )
    row_count = merged.shape[0]
    head_count = grad_rows.shape[1] // HD
    pair_width = head_count * 2 * HD
    per_head = merged.reshape(row_count, head_count, 3, HD)
    query_rows = per_head[:, :, 0]
    pair_rows = per_head[:, :, 1:].reshape(row_count, pair_width)
    shard_index = lax.axis_index("ctx")
    total_blocks = SEARCHER_TILES * lax.axis_size("ctx")
    local_ids = shard_index * SEARCHER_TILES + jnp.arange(SEARCHER_TILES, dtype=jnp.int32)
    window = local_ids[:, None] - 1 + jnp.arange(3, dtype=jnp.int32)[None, :]
    window_ok = (window >= 0) & (window < total_blocks)
    listed_ok = jnp.arange(DRAWN_TARGET_SET, dtype=jnp.int32)[None, :] < live_counts[:, None]
    usable = jnp.concatenate([window_ok, listed_ok], axis=1)
    offsets = [offset for offset in range(-SPAN, SPAN + 1) if offset != 0]
    owner_tables = []
    rims = extended_2(pair_rows, (("ctx", 0),), BLK)
    pieces = [rims]
    rank_list = []
    own_blocks = pair_rows.reshape(SEARCHER_TILES, BLK, pair_width)
    for offset in offsets:
        wanted = needed_blocks(key_lists, shard_index + offset)
        rank_list.append(slot_numbers(wanted))
        theirs = from_behind(key_lists, "ctx", offset)
        owner_table = select_table(needed_blocks(theirs, shard_index))
        owner_tables.append(owner_table)
        outgoing = jnp.einsum(
            "st,tbf->sbf",
            owner_table.astype(jnp.bfloat16),
            own_blocks,
            preferred_element_type=jnp.float32,
        )
        outgoing = outgoing.astype(jnp.bfloat16).reshape(NAMED_TILE_LIMIT * BLK, pair_width)
        pieces.append(from_behind(outgoing, "ctx", -offset))
    extended = jnp.concatenate(pieces, axis=0)
    rank_table = jnp.stack(rank_list)
    gap_shard = key_lists // SEARCHER_TILES - shard_index
    block_in = key_lists % SEARCHER_TILES
    side_of = jnp.where(gap_shard < 0, gap_shard + SPAN, gap_shard + SPAN - 1)
    side_hit = side_of[:, :, None] == jnp.arange(2 * SPAN, dtype=jnp.int32)[None, None, :]
    block_hit = block_in[:, :, None] == jnp.arange(SEARCHER_TILES, dtype=jnp.int32)[None, None, :]
    rank_here = jnp.sum(
        jnp.where(side_hit[:, :, :, None] & block_hit[:, :, None, :], rank_table[None, None], 0),
        axis=(2, 3),
    )
    far_place = SEARCHER_TILES + 2 + side_of * NAMED_TILE_LIMIT + rank_here
    listed_place = jnp.where(gap_shard == 0, 1 + block_in, far_place)
    window_place = jnp.clip(window - shard_index * SEARCHER_TILES + 1, 0, SEARCHER_TILES + 1)
    places = jnp.concatenate([window_place, listed_place], axis=1)
    block_count = extended.shape[0] // BLK
    tile_ordinals = extended.reshape(block_count, BLK, head_count, 2, HD)
    query_blocks = query_rows.reshape(SEARCHER_TILES, BLK, head_count, HD)
    grad_blocks = grad_rows.reshape(SEARCHER_TILES, BLK, head_count, HD)

    def step(carry, inputs):
        query_part, grad_part, block_places, block_ok = inputs
        chosen = tile_ordinals[block_places]
        grad_query, grad_pairs = block_grads(
            query_part, grad_part, chosen[:, :, :, 0], chosen[:, :, :, 1], block_ok
        )
        return (carry, (grad_query, grad_pairs))

    carry_zero = jnp.zeros((), jnp.float32)
    carry_zero, outputs = lax.scan(step, carry_zero, (query_blocks, grad_blocks, places, usable))
    grad_query, pair_terms = outputs
    slot_total = pair_terms.shape[0] * pair_terms.shape[1]
    flat_terms = pair_terms.reshape(slot_total, BLK * pair_width)
    place_flat = places.reshape(slot_total)
    owner_hits = (place_flat[None, :] == jnp.arange(block_count, dtype=jnp.int32)[:, None]).astype(
        jnp.float32
    )
    totals = jnp.dot(
        owner_hits, flat_terms, precision=lax.Precision.HIGHEST, preferred_element_type=jnp.float32
    )
    totals = totals.reshape(block_count, BLK, pair_width)
    own_grads = totals[1 : SEARCHER_TILES + 1]
    for direction in (-1, 1):
        rim_rows = totals[0] if direction == -1 else totals[SEARCHER_TILES + 1]
        arrived = from_behind(rim_rows.astype(jnp.bfloat16), "ctx", direction).astype(
            rim_rows.dtype
        )
        target_block = SEARCHER_TILES - 1 if direction == -1 else 0
        own_grads = own_grads.at[target_block].add(arrived)
    for side_index, offset in enumerate(offsets):
        first_slot = SEARCHER_TILES + 2 + side_index * NAMED_TILE_LIMIT
        arrived = from_behind(totals[first_slot : first_slot + NAMED_TILE_LIMIT], "ctx", offset)
        own_grads = own_grads + jnp.einsum(
            "st,sbf->tbf", owner_tables[side_index], arrived, precision=lax.Precision.HIGHEST
        )
    own_grads = own_grads.reshape(SEARCHER_TILES, BLK, head_count, 2, HD)
    joined = jnp.concatenate([grad_query[:, :, :, None, :], own_grads], axis=3)
    joined = joined.astype(jnp.bfloat16).reshape(row_count, head_count * 3 * HD)
    return lax.all_to_all(joined, "head", split_axis=0, concat_axis=1, tiled=True)


def solution(mesh):
    placed = (P(("ctx", "head"), None), P(("ctx", "head"), None), P("ctx", None), P("ctx"))
    return jax.shard_map(
        shards, mesh=mesh, in_specs=placed, out_specs=P(("ctx", "head"), None), check_vma=False
    )
```

profile of v0, /device:TPU:0, one launch (start us, length us, event | category | flops | bytes accessed | tf_op | source)
XLA Modules:
  0.0 669.3 jit_solution(15242273154368790769)
XLA Ops:
  24.3 32.0 %all-to-all-done = bf16[128,4,3072]{0,2,1:T(8,128)(2,1)S(1)} async-done(((bf16[128,4,3072]{0,2,1:T(8,128)(2,1)}), bf16[128,4,3072]{0,2,1:T(8,128)(2,1)S(1)}, u32[]{:S(2)}, u32[]{:S(2)}) %all-to-all-start) | async-done | bytes 3145760 | tf_op jit(solution)/shard_map/all_to_all | solution.py:89
  60.6 15.6 %copy.139 = bf16[4,128,3072]{1,0,2:T(4,128)(2,1)} copy(bf16[4,128,3072]{1,2,0:T(8,128)(2,1)S(1)} %bitcast.205) | data formatting | bytes 6291456 | tf_op jit(solution)/shard_map/all_to_all | solution.py:89
  86.0 5.5 collective-permute-start
  105.6 6.9 %collective-permute-start.3 = (bf16[256,2048]{1,0:T(8,128)(2,1)}, bf16[256,2048]{1,0:T(8,128)(2,1)}, u32[]{:S(2)}, u32[]{:S(2)}) collective-permute-start(bf16[256,2048]{1,0:T(8,128)(2,1)} %bitcast.34), channel_id=1, source_target_pairs={{0,8},{4,12},{8,16},{12,20},{16,24},{20,28},{1,9},{5,13},{9,17},{1... | collective-permute-start | bytes 3145736 | tf_op jit(solution)/shard_map/ppermute | solution.py:34
  137.7 25.6 %collective-permute-done.5 = bf16[256,2048]{1,0:T(8,128)(2,1)} collective-permute-done((bf16[256,2048]{1,0:T(8,128)(2,1)}, bf16[256,2048]{1,0:T(8,128)(2,1)}, u32[]{:S(2)}, u32[]{:S(2)}) %collective-permute-start.5) | collective-permute-done | bytes 1048608 | tf_op jit(solution)/shard_map/ppermute | solution.py:34
  172.1 12.6 %reshape.229 = bf16[14,128,8,2,128]{4,3,2,1,0:T(2,128)(2,1)} reshape(bf16[1792,2048]{1,0:T(8,128)(2,1)} %constant_dynamic-update-slice_fusion) | data formatting | bytes 14680064 | tf_op jit(solution)/shard_map/reshape | solution.py:141
  184.7 7.5 %copy.154 = bf16[14,128,8,2,128]{4,2,3,1,0:T(8,128)(2,1)} copy(bf16[14,128,8,2,128]{4,3,2,1,0:T(2,128)(2,1)} %reshape.229) | data formatting | bytes 14680064 | tf_op jit(solution)/shard_map/while | solution.py:154
  192.2 143.2 %while.14 = (s32[]{:T(128)}, bf16[4,128,8,128]{1,3,2,0:T(8,128)(2,1)S(1)}, f32[4,7,128,8,2,128]{5,4,3,2,1,0:T(2,128)}, s32[4,7]{1,0:T(4,128)S(1)}, bf16[14,128,8...) while((s32[]{:T(128)}, ...), condition=%wide.region_21.22_spmd, body=%wide.region_17.21_spmd.sunk | while | flops 1203894272 | bytes 104907184 | solution.py:154
  192.6 6.1 gather_fusion
  216.6 11.7 %copy_dynamic-update-slice_fusion.2 = f32[4,7,128,8,2,128]{5,4,3,2,1,0:T(2,128)} fusion(f32[4,7,128,8,2,128]{5,4,3,2,1,0:T(2,128)} %get-tuple-element.224, s32[]{:T(128)S(6)} %copy.226, f32[1,7,128,8,2,128]{5,2,1,3,4,0:T(8,128)} %maximum_bitcast_fusion.2), kind=kLoop, calls=%fused_computation.2.clone.1 | loop fusion | bytes 14680068 | tf_op jit(solution)/shard_map/while/body/jit(dynamic_update_index_in_dim)/dynamic_update_slice | solution.py:154
  228.2 6.1 gather_fusion
  252.2 11.8 %copy_dynamic-update-slice_fusion.2 = f32[4,7,128,8,2,128]{5,4,3,2,1,0:T(2,128)} fusion(f32[4,7,128,8,2,128]{5,4,3,2,1,0:T(2,128)} %get-tuple-element.224, s32[]{:T(128)S(6)} %copy.226, f32[1,7,128,8,2,128]{5,2,1,3,4,0:T(8,128)} %maximum_bitcast_fusion.2), kind=kLoop, calls=%fused_computation.2.clone.1 | loop fusion | bytes 14680068 | tf_op jit(solution)/shard_map/while/body/jit(dynamic_update_index_in_dim)/dynamic_update_slice | solution.py:154
  264.0 6.1 gather_fusion
  287.9 11.8 %copy_dynamic-update-slice_fusion.2 = f32[4,7,128,8,2,128]{5,4,3,2,1,0:T(2,128)} fusion(f32[4,7,128,8,2,128]{5,4,3,2,1,0:T(2,128)} %get-tuple-element.224, s32[]{:T(128)S(6)} %copy.226, f32[1,7,128,8,2,128]{5,2,1,3,4,0:T(8,128)} %maximum_bitcast_fusion.2), kind=kLoop, calls=%fused_computation.2.clone.1 | loop fusion | bytes 14680068 | tf_op jit(solution)/shard_map/while/body/jit(dynamic_update_index_in_dim)/dynamic_update_slice | solution.py:154
  299.7 6.1 gather_fusion
  323.6 11.7 %copy_dynamic-update-slice_fusion.2 = f32[4,7,128,8,2,128]{5,4,3,2,1,0:T(2,128)} fusion(f32[4,7,128,8,2,128]{5,4,3,2,1,0:T(2,128)} %get-tuple-element.224, s32[]{:T(128)S(6)} %copy.226, f32[1,7,128,8,2,128]{5,2,1,3,4,0:T(8,128)} %maximum_bitcast_fusion.2), kind=kLoop, calls=%fused_computation.2.clone.1 | loop fusion | bytes 14680068 | tf_op jit(solution)/shard_map/while/body/jit(dynamic_update_index_in_dim)/dynamic_update_slice | solution.py:154
  335.4 51.0 %reshape.231 = f32[28,262144]{1,0:T(8,128)} reshape(f32[4,7,128,8,2,128]{5,4,3,2,1,0:T(2,128)} %get-tuple-element.73) | data formatting | bytes 58720256 | tf_op jit(solution)/shard_map/reshape | solution.py:157
  386.4 25.8 %fusion.84 = (bf16[14,262144]{1,0:T(8,128)(2,1)}, f32[14,262144]{1,0:T(8,128)}) fusion(f32[28,262144]{1,0:T(8,128)} %reshape.231, s32[28]{0:T(128)S(1)} %copy-done.27), kind=kOutput, calls=%fused_computation.152 | convolution fusion | flops 1236795776 | bytes 51380336 | tf_op jit(solution)/shard_map/dot_general | solution.py:162
  412.2 15.1 %fusion.82 = (f32[2,262144]{1,0:T(2,128)}, f32[2,262144]{1,0:T(2,128)}, f32[2,262144]{1,0:T(2,128)}, f32[2,262144]{1,0:T(2,128)}) fusion(f32[14,262144]{1,0:T(8,128)} %get-tuple-element.145), kind=kLoop, calls=%fused_computation.150 | loop fusion | bytes 16777216 | tf_op jit(solution)/shard_map/slice | solution.py:176
  431.3 13.9 %slice_reduce_fusion = (bf16[262144]{0:T(1024)(128)(2,1)S(1)}, bf16[262144]{0:T(1024)(128)(2,1)S(1)}) fusion(bf16[14,262144]{1,0:T(8,128)(2,1)} %get-tuple-element.144), kind=kLoop, calls=%fused_computation.47 | loop fusion | bytes 2097152 | tf_op jit(solution)/shard_map/slice | solution.py:168
  447.7 7.5 %collective-permute-start.11 = (bf16[128,2048]{1,0:T(8,128)(2,1)}, bf16[128,2048]{1,0:T(8,128)(2,1)}, u32[]{:S(2)}, u32[]{:S(2)}) collective-permute-start(bf16[128,2048]{1,0:T(8,128)(2,1)} %convert_element_type.88), channel_id=1, source_target_pairs={{0,4},{4,8},{8,12},{12,16},{16,20},{20,24},{24,28},{1,5},{5,9},{9,... | collective-permute-start | bytes 1572872 | tf_op jit(solution)/shard_map/ppermute | solution.py:34
  456.5 13.2 %slice_reduce_fusion.2 = f32[262144]{0:T(1024)S(1)} fusion(f32[14,262144]{1,0:T(8,128)} %get-tuple-element.145), kind=kLoop, calls=%fused_computation.50 | loop fusion | bytes 2097152 | tf_op jit(solution)/shard_map/slice.64
  469.7 5.2 slice.140
  475.1 16.0 %collective-permute-done.10 = bf16[128,2048]{1,0:T(8,128)(2,1)S(1)} collective-permute-done((bf16[128,2048]{1,0:T(8,128)(2,1)S(1)}, bf16[128,2048]{1,0:T(8,128)(2,1)S(1)}, u32[]{:S(2)}, u32[]{:S(2)}) %collective-permute-start.10) | collective-permute-done | bytes 524320 | tf_op jit(solution)/shard_map/ppermute | solution.py:34
  491.9 57.7 %collective-permute-start.15 = (f32[2,128,2048]{2,0,1:T(2,128)}, f32[2,128,2048]{2,0,1:T(2,128)S(1)}, u32[]{:S(2)}, u32[]{:S(2)}) collective-permute-start(f32[2,128,2048]{2,0,1:T(2,128)} %bitcast.214), channel_id=1, source_target_pairs={{0,8},{4,12},{8,16},{12,20},{16,24},{20,28},{1,9},{5,13},{9,17},{1... | collective-permute-start | bytes 6291464 | tf_op jit(solution)/shard_map/ppermute | solution.py:34
  551.5 19.9 %scatter-add.6 = f32[4,128,2048]{2,0,1:T(4,128)} dynamic-update-slice(f32[4,128,2048]{2,0,1:T(4,128)} %bitcast.203, f32[1,128,2048]{2,0,1:T(1,128)S(1)} %add.185, s32[]{:T(128)} %constant.137.clone.1, s32[]{:T(128)} %constant.129.clone.1, s32[]{:T(128)} %constant.129.clone.1) | dynamic-update-slice | bytes 2097156 | tf_op jit(solution)/shard_map/scatter-add | solution.py:173
  575.4 19.5 %scatter-add.9 = f32[4,128,2048]{2,0,1:T(4,128)} dynamic-update-slice(f32[4,128,2048]{2,0,1:T(4,128)} %scatter-add.6, f32[1,128,2048]{2,0,1:T(1,128)S(1)} %slice_add_fusion, s32[]{:T(128)} %constant.129.clone.1, s32[]{:T(128)} %constant.129.clone.1, s32[]{:T(128)} %constant.129.clone.1) | dynamic-update-slice | bytes 2097156 | tf_op jit(solution)/shard_map/scatter-add | solution.py:173
  594.9 6.4 fusion.54
  601.4 6.4 fusion.56
  607.8 6.5 fusion.58
  614.4 8.7 %add_convert_fusion = bf16[4,128,2048]{2,0,1:T(4,128)(2,1)} fusion(f32[4,128,2048]{2,0,1:T(4,128)S(1)} %fusion.54, f32[4,128,2048]{2,0,1:T(4,128)S(1)} %fusion.56, f32[4,128,2048]{2,0,1:T(4,128)S(1)} %copy-done, f32[4,128,2048]{2,0,1:T(4,128)S(1)} %fusion.58, f32[2,128,2048]{2,0,1:T(2,128)S(1)} %collective-permute-done.15, pred[4]{0:T(512)(128)(4,1)S(1)} %copy-done.12, ...), kind=kOutput, calls=%fused_computation.41 | convolution fusion | flops 30408720 | bytes 20971540 | tf_op jit(solution)/shard_map/st,sbf->tbf/dot_general | solution.py:177
  626.9 39.4 %all_to_all.48 = bf16[4,128,3072]{1,2,0:T(8,128)(2,1)S(1)} all-to-all(bf16[4,128,3072]{1,2,0:T(8,128)(2,1)S(1)} %bitcast.207), channel_id=1, replica_groups=mesh['ctx'=8,'head'=4] {'head'}, dimensions={0} | all-to-all | bytes 6291456 | tf_op jit(solution)/shard_map/all_to_all | solution.py:183
  (218 shorter events, 178.6 us)
Async XLA Ops:
  0.0 23.8 %collective-permute-start.8 = (s32[4,4]{1,0:T(4,128)}, s32[4,4]{1,0:T(4,128)S(1)}, u32[]{:S(2)}, u32[]{:S(2)}) collective-permute-start(s32[4,4]{1,0:T(4,128)} %param.12), channel_id=1, source_target_pairs={{0,8},{4,12},{8,16},{12,20},{16,24},{20,28},{1,9},{5,13},{9,17},{1... | collective-permute-start | bytes 200 | tf_op jit(solution)/shard_map/ppermute | solution.py:34
  5.0 18.9 %collective-permute-start.6 = (s32[4,4]{1,0:T(4,128)}, s32[4,4]{1,0:T(4,128)S(1)}, u32[]{:S(2)}, u32[]{:S(2)}) collective-permute-start(s32[4,4]{1,0:T(4,128)} %param.12), channel_id=1, source_target_pairs={{0,4},{4,8},{8,12},{12,16},{16,20},{20,24},{24,28},{1,5},{5,9},{9,... | collective-permute-start | bytes 200 | tf_op jit(solution)/shard_map/ppermute | solution.py:34
  8.4 15.5 %collective-permute-start.2 = (s32[4,4]{1,0:T(4,128)}, s32[4,4]{1,0:T(4,128)S(1)}, u32[]{:S(2)}, u32[]{:S(2)}) collective-permute-start(s32[4,4]{1,0:T(4,128)} %param.12), channel_id=1, source_target_pairs={{8,0},{12,4},{16,8},{20,12},{24,16},{28,20},{9,1},{13,5},{17,9},{2... | collective-permute-start | bytes 200 | tf_op jit(solution)/shard_map/ppermute | solution.py:34
  9.7 14.2 %collective-permute-start.4 = (s32[4,4]{1,0:T(4,128)}, s32[4,4]{1,0:T(4,128)S(1)}, u32[]{:S(2)}, u32[]{:S(2)}) collective-permute-start(s32[4,4]{1,0:T(4,128)} %param.12), channel_id=1, source_target_pairs={{4,0},{8,4},{12,8},{16,12},{20,16},{24,20},{28,24},{5,1},{9,5},{13... | collective-permute-start | bytes 200 | tf_op jit(solution)/shard_map/ppermute | solution.py:34
  15.6 40.7 %all-to-all-start = ((bf16[128,4,3072]{0,2,1:T(8,128)(2,1)}), bf16[128,4,3072]{0,2,1:T(8,128)(2,1)S(1)}, u32[]{:S(2)}, u32[]{:S(2)}) async-start(bf16[128,4,3072]{0,2,1:T(8,128)(2,1)} %bitcast.206), calls=%async_computation | async-start | bytes 6291456 | tf_op jit(solution)/shard_map/all_to_all | solution.py:89
  23.9 79.0 %copy-start.13 = (pred[4]{0:T(512)(128)(4,1)}, pred[4]{0:T(512)(128)(4,1)S(1)}, u32[]{:S(2)}) copy-start(pred[4]{0:T(512)(128)(4,1)S(1)} %get-tuple-element.114) | copy-start | bytes 16
  23.9 88.5 %copy-start.15 = (pred[4]{0:T(512)(128)(4,1)}, pred[4]{0:T(512)(128)(4,1)S(1)}, u32[]{:S(2)}) copy-start(pred[4]{0:T(512)(128)(4,1)S(1)} %get-tuple-element.115) | copy-start | bytes 16
  24.0 95.2 %copy-start.17 = (pred[4]{0:T(512)(128)(4,1)}, pred[4]{0:T(512)(128)(4,1)S(1)}, u32[]{:S(2)}) copy-start(pred[4]{0:T(512)(128)(4,1)S(1)} %get-tuple-element.113) | copy-start | bytes 16
  24.0 99.1 %copy-start.11 = (pred[4]{0:T(512)(128)(4,1)}, pred[4]{0:T(512)(128)(4,1)S(1)}, u32[]{:S(2)}) copy-start(pred[4]{0:T(512)(128)(4,1)S(1)} %get-tuple-element.112) | copy-start | bytes 16
  24.1 78.9 %copy-start.21 = (s32[4]{0:T(128)}, s32[4]{0:T(128)S(1)}, u32[]{:S(2)}) copy-start(s32[4]{0:T(128)S(1)} %get-tuple-element.155) | copy-start | bytes 52
  24.1 88.3 %copy-start.23 = (s32[4]{0:T(128)}, s32[4]{0:T(128)S(1)}, u32[]{:S(2)}) copy-start(s32[4]{0:T(128)S(1)} %get-tuple-element.154) | copy-start | bytes 52
  24.3 94.9 %copy-start.25 = (s32[4]{0:T(128)}, s32[4]{0:T(128)S(1)}, u32[]{:S(2)}) copy-start(s32[4]{0:T(128)S(1)} %get-tuple-element.153) | copy-start | bytes 52
  24.3 98.8 %copy-start.19 = (s32[4]{0:T(128)}, s32[4]{0:T(128)S(1)}, u32[]{:S(2)}) copy-start(s32[4]{0:T(128)S(1)} %get-tuple-element.152) | copy-start | bytes 52
  56.3 135.9 %all-to-all-start.1 = ((bf16[128,4,1024]{0,2,1:T(8,128)(2,1)}), bf16[128,4,1024]{0,2,1:T(8,128)(2,1)}, u32[]{:S(2)}, u32[]{:S(2)}) async-start(bf16[128,4,1024]{0,2,1:T(8,128)(2,1)} %bitcast.211), calls=%async_computation.1 | async-start | bytes 2097152 | tf_op jit(solution)/shard_map/all_to_all | solution.py:90
  86.0 10.0 %copy-start.4 = (bf16[128,8,2,128]{0,3,2,1:T(8,128)(2,1)S(1)}, bf16[128,8,2,128]{0,3,2,1:T(8,128)(2,1)}, u32[]{:S(2)}) copy-start(bf16[128,8,2,128]{0,3,2,1:T(8,128)(2,1)} %get-tuple-element.140) | copy-start | bytes 1572868
  86.0 42.9 %collective-permute-start = (bf16[128,2048]{1,0:T(8,128)(2,1)}, bf16[128,2048]{1,0:T(8,128)(2,1)}, u32[]{:S(2)}, u32[]{:S(2)}) collective-permute-start(bf16[128,2048]{1,0:T(8,128)(2,1)} %copy.140), channel_id=1, source_target_pairs={{0,4},{4,8},{8,12},{12,16},{16,20},{20,24},{24,28},{1,5},{5,9},{9,... | collective-permute-start | bytes 1572872 | tf_op jit(solution)/shard_map/ppermute | solution.py:22
  97.0 36.5 %collective-permute-start.1 = (bf16[128,2048]{1,0:T(8,128)(2,1)}, bf16[128,2048]{1,0:T(8,128)(2,1)}, u32[]{:S(2)}, u32[]{:S(2)}) collective-permute-start(bf16[128,2048]{1,0:T(8,128)(2,1)} %copy.141), channel_id=1, source_target_pairs={{4,0},{8,4},{12,8},{16,12},{20,16},{24,20},{28,24},{5,1},{9,5},{13... | collective-permute-start | bytes 1572872 | tf_op jit(solution)/shard_map/ppermute | solution.py:24
  103.0 16.2 %copy-start.3 = (bf16[4,128,2048]{2,0,1:T(4,128)(2,1)}, bf16[4,128,2048]{2,0,1:T(4,128)(2,1)S(1)}, u32[]{:S(2)}) copy-start(bf16[4,128,2048]{2,0,1:T(4,128)(2,1)S(1)} %copy.143) | copy-start | bytes 6291460
  105.6 29.9 %collective-permute-start.3 = (bf16[256,2048]{1,0:T(8,128)(2,1)}, bf16[256,2048]{1,0:T(8,128)(2,1)}, u32[]{:S(2)}, u32[]{:S(2)}) collective-permute-start(bf16[256,2048]{1,0:T(8,128)(2,1)} %bitcast.34), channel_id=1, source_target_pairs={{0,8},{4,12},{8,16},{12,20},{16,24},{20,28},{1,9},{5,13},{9,17},{1... | collective-permute-start | bytes 3145736 | tf_op jit(solution)/shard_map/ppermute | solution.py:34
  115.0 48.3 %collective-permute-start.5 = (bf16[256,2048]{1,0:T(8,128)(2,1)}, bf16[256,2048]{1,0:T(8,128)(2,1)}, u32[]{:S(2)}, u32[]{:S(2)}) collective-permute-start(bf16[256,2048]{1,0:T(8,128)(2,1)} %bitcast.36), channel_id=1, source_target_pairs={{0,4},{4,8},{8,12},{12,16},{16,20},{20,24},{24,28},{1,5},{5,9},{9,... | collective-permute-start | bytes 3145736 | tf_op jit(solution)/shard_map/ppermute | solution.py:34
  121.8 43.9 %collective-permute-start.7 = (bf16[256,2048]{1,0:T(8,128)(2,1)}, bf16[256,2048]{1,0:T(8,128)(2,1)}, u32[]{:S(2)}, u32[]{:S(2)}) collective-permute-start(bf16[256,2048]{1,0:T(8,128)(2,1)} %bitcast.38), channel_id=1, source_target_pairs={{4,0},{8,4},{12,8},{16,12},{20,16},{24,20},{28,24},{5,1},{9,5},{13... | collective-permute-start | bytes 3145736 | tf_op jit(solution)/shard_map/ppermute | solution.py:34
  128.9 42.2 %collective-permute-start.9 = (bf16[256,2048]{1,0:T(8,128)(2,1)}, bf16[256,2048]{1,0:T(8,128)(2,1)S(1)}, u32[]{:S(2)}, u32[]{:S(2)}) collective-permute-start(bf16[256,2048]{1,0:T(8,128)(2,1)} %bitcast.215), channel_id=1, source_target_pairs={{8,0},{12,4},{16,8},{20,12},{24,16},{28,20},{9,1},{13,5},{17,9},{2... | collective-permute-start | bytes 3145736 | tf_op jit(solution)/shard_map/ppermute | solution.py:34
  335.4 51.0 %copy-start.7 = (bf16[4,128,8,128]{1,3,2,0:T(8,128)(2,1)}, bf16[4,128,8,128]{1,3,2,0:T(8,128)(2,1)S(1)}, u32[]{:S(2)}) copy-start(bf16[4,128,8,128]{1,3,2,0:T(8,128)(2,1)S(1)} %get-tuple-element.72) | copy-start | bytes 3145732
  335.4 51.0 %copy-start.27 = (s32[28]{0:T(128)S(1)}, s32[28]{0:T(128)}, u32[]{:S(2)}) copy-start(s32[28]{0:T(128)} %eq.235) | copy-start | bytes 340
  427.3 167.6 %collective-permute-start.14 = (f32[2,128,2048]{2,0,1:T(2,128)}, f32[2,128,2048]{2,0,1:T(2,128)}, u32[]{:S(2)}, u32[]{:S(2)}) collective-permute-start(f32[2,128,2048]{2,0,1:T(2,128)} %bitcast.52), channel_id=1, source_target_pairs={{0,4},{4,8},{8,12},{12,16},{16,20},{20,24},{24,28},{1,5},{5,9},{9,... | collective-permute-start | bytes 6291464 | tf_op jit(solution)/shard_map/ppermute | solution.py:34
  430.0 171.4 %collective-permute-start.13 = (f32[2,128,2048]{2,0,1:T(2,128)}, f32[2,128,2048]{2,0,1:T(2,128)}, u32[]{:S(2)}, u32[]{:S(2)}) collective-permute-start(f32[2,128,2048]{2,0,1:T(2,128)} %bitcast.50), channel_id=1, source_target_pairs={{4,0},{8,4},{12,8},{16,12},{20,16},{24,20},{28,24},{5,1},{9,5},{13... | collective-permute-start | bytes 6291464 | tf_op jit(solution)/shard_map/ppermute | solution.py:34
  445.4 45.7 %collective-permute-start.10 = (bf16[128,2048]{1,0:T(8,128)(2,1)S(1)}, bf16[128,2048]{1,0:T(8,128)(2,1)S(1)}, u32[]{:S(2)}, u32[]{:S(2)}) collective-permute-start(bf16[128,2048]{1,0:T(8,128)(2,1)S(1)} %convert_element_type.86), channel_id=1, source_target_pairs={{4,0},{8,4},{12,8},{16,12},{20,16},{24,20},{28,24},{5,1},{9,5},{13... | collective-permute-start | bytes 1572872 | tf_op jit(solution)/shard_map/ppermute | solution.py:34
  447.7 123.7 %collective-permute-start.11 = (bf16[128,2048]{1,0:T(8,128)(2,1)}, bf16[128,2048]{1,0:T(8,128)(2,1)}, u32[]{:S(2)}, u32[]{:S(2)}) collective-permute-start(bf16[128,2048]{1,0:T(8,128)(2,1)} %convert_element_type.88), channel_id=1, source_target_pairs={{0,4},{4,8},{8,12},{12,16},{16,20},{20,24},{24,28},{1,5},{5,9},{9,... | collective-permute-start | bytes 1572872 | tf_op jit(solution)/shard_map/ppermute | solution.py:34
  455.2 152.6 %collective-permute-start.12 = (f32[2,128,2048]{2,0,1:T(2,128)}, f32[2,128,2048]{2,0,1:T(2,128)}, u32[]{:S(2)}, u32[]{:S(2)}) collective-permute-start(f32[2,128,2048]{2,0,1:T(2,128)} %bitcast.48), channel_id=1, source_target_pairs={{8,0},{12,4},{16,8},{20,12},{24,16},{28,20},{9,1},{13,5},{17,9},{2... | collective-permute-start | bytes 6291464 | tf_op jit(solution)/shard_map/ppermute | solution.py:34
  491.9 122.5 %collective-permute-start.15 = (f32[2,128,2048]{2,0,1:T(2,128)}, f32[2,128,2048]{2,0,1:T(2,128)S(1)}, u32[]{:S(2)}, u32[]{:S(2)}) collective-permute-start(f32[2,128,2048]{2,0,1:T(2,128)} %bitcast.214), channel_id=1, source_target_pairs={{0,8},{4,12},{8,16},{12,20},{16,24},{20,28},{1,9},{5,13},{9,17},{1... | collective-permute-start | bytes 6291464 | tf_op jit(solution)/shard_map/ppermute | solution.py:34
  571.4 23.5 %copy-start.18 = (pred[4]{0:T(512)(128)(4,1)S(1)}, pred[4]{0:T(512)(128)(4,1)}, u32[]{:S(2)}) copy-start(pred[4]{0:T(512)(128)(4,1)} %copy-done.17) | copy-start | bytes 16
  571.4 23.5 %copy-start.26 = (s32[4]{0:T(128)S(1)}, s32[4]{0:T(128)}, u32[]{:S(2)}) copy-start(s32[4]{0:T(128)} %copy-done.25) | copy-start | bytes 52
  (16 other events, 87.4 us)
where the time goes:
time: 681 us; the launch traced here: 669 us
  local copies, waits for them, and re-layouts  318 us (47%)
  starting transfers between devices  111 us (16%)
  matrix products  83.8 us (12%)
  waiting for transfers between devices  76.7 us (11%)
  blocking collectives  39.4 us (6%)
  other arithmetic  38.5 us (6%)
    ppermute x14, starting transfers between devices, from_behind(): lax.ppermute(value, axis, [(source, source + steps) for source in range(i...  96.3 us
    reshape x1, local copies, waits for them, and re-layouts, shards(): flat_terms = pair_terms.reshape(slot_total, BLK * pair_width)  51 us
    dynamic_update_slice x4, local copies, waits for them, and re-layouts, shards(): lax.scan(step, carry_zero, (query_blocks, grad_blocks, places, usable))  46.9 us
    ppermute x14, waiting for transfers between devices, from_behind(): lax.ppermute(value, axis, [(source, source + steps) for source in range(i...  44.7 us
    all_to_all x1, blocking collectives, shards(): lax.all_to_all(joined, 'head', split_axis=0, concat_axis=1, tiled=True)  39.4 us
    scatter-add x2, local copies, waits for them, and re-layouts, shards(): own_grads = own_grads.at[target_block].add(arrived)  39.4 us
    all_to_all x1, waiting for transfers between devices, shards(): lax.all_to_all(qkv, 'head', split_axis=1, concat_axis=0, tiled=True)  32 us
    dot_general x4, matrix products, shards(): jnp.einsum('st,sbf->tbf', owner_tables[side_index], arrived, precision=la...  28 us
  transfers between devices with their start and end apart: 18, of which 4 were waited for; matrix products, arithmetic and copies ran while one was open for 28% of the time, Pallas kernels for 0%

commit v1 on v0

v1 whole, which is shorter than its diff:
```python
import functools

import jax
import jax.numpy as jnp
from jax import lax
from jax.experimental import pallas as pl
from jax.experimental.pallas import tpu as pltpu
from jax.sharding import Mesh, PartitionSpec as P

HD = 128
BLK = 128
TILES = 4
LISTED = 4
NAMED = 2
PAIR = 2 * TILES
EDGE = NAMED + TILES
ALL = 2 * EDGE + PAIR
SCALE = HD ** (-0.5)
CHUNKS = 2
F32 = jnp.float32
BF16 = jnp.bfloat16


def rows(block, count=1):
    start = block * BLK
    return pl.ds(start if isinstance(start, int) else pl.multiple_of(start, BLK), count * BLK)


def pack_kernel(slots, own, to_next, to_prev):
    for s in range(NAMED):
        to_next[rows(s), :] = own[rows(slots[0, s]), HD:]
        to_prev[rows(TILES + s), :] = own[rows(TILES + slots[1, s]), HD:]
    to_next[rows(NAMED, TILES), :] = own[rows(TILES, TILES), HD:]
    to_prev[rows(0, TILES), :] = own[rows(0, TILES), HD:]


def attention_kernel(places, info, own, grads, left, right, dq, own_grads, left_grads, right_grads, pairs, acc):
    pairs[rows(0, EDGE), :] = left[...]
    pairs[rows(EDGE, PAIR), :] = own[:, HD:]
    pairs[rows(EDGE + PAIR, EDGE), :] = right[...]
    acc[...] = jnp.zeros_like(acc)

    def step(i, carry):
        q = own[rows(i), :HD]
        g = grads[rows(i), :]
        zero = jnp.zeros_like(q)
        both = jnp.concatenate(
            [jnp.concatenate([q, zero], axis=1), jnp.concatenate([zero, g], axis=1)], axis=0
        )
        where = [EDGE - 1 + i + n for n in range(3)] + [places[i, j] for j in range(LISTED)]
        live = info[0, i]
        usable = [info[1, i] > 0, None, info[2, i] > 0] + [live > j for j in range(LISTED)]
        kv = jnp.concatenate([pairs[rows(p), :] for p in where], axis=0)
        products = lax.dot_general(kv, both, (((1,), (1,)), ((), ())), preferred_element_type=F32)
        scores = []
        for n, ok in enumerate(usable):
            s = products[n * BLK : (n + 1) * BLK, :HD] * SCALE
            scores.append(s if ok is None else jnp.where(ok, s, -1e30))
        scores = jnp.concatenate(scores, axis=0)
        powers = jnp.exp(scores - jnp.max(scores, axis=0, keepdims=True))
        soft = powers * (1.0 / jnp.sum(powers, axis=0, keepdims=True))
        dp = products[:, HD:]
        ds = soft * (dp - jnp.sum(soft * dp, axis=0, keepdims=True))
        ds_low = ds.astype(BF16)
        low = jnp.concatenate([ds_low, soft.astype(BF16)], axis=1)
        terms = jnp.dot(low, both, preferred_element_type=F32)
        grad_q = lax.dot_general(ds_low, kv[:, :HD], (((0,), (0,)), ((), ())), preferred_element_type=F32)
        dq[rows(i), :] = (grad_q * SCALE).astype(BF16)
        acc[rows(EDGE - 1 + i, 3), :] += terms[: 3 * BLK]
        for j in range(LISTED):
            acc[rows(where[3 + j]), :] += terms[(3 + j) * BLK : (4 + j) * BLK]
        return carry

    lax.fori_loop(0, PAIR, step, 0)
    for k, factor in ((0, SCALE), (HD, 1.0)):
        columns = slice(k, k + HD)
        own_grads[:, columns] = acc[rows(EDGE, PAIR), columns] * factor
        left_grads[:, columns] = (acc[rows(0, EDGE), columns] * factor).astype(BF16)
        right_grads[:, columns] = (acc[rows(EDGE + PAIR, EDGE), columns] * factor).astype(BF16)


def combine_kernel(slots, dq, own_grads, from_next, from_prev, out, acc):
    acc[...] = own_grads[...]
    acc[rows(TILES, TILES), :] += from_next[rows(NAMED, TILES), :].astype(F32)
    acc[rows(0, TILES), :] += from_prev[rows(0, TILES), :].astype(F32)
    for s in range(NAMED):
        acc[rows(slots[0, s]), :] += from_next[rows(s), :].astype(F32)
        acc[rows(TILES + slots[1, s]), :] += from_prev[rows(TILES + s), :].astype(F32)
    out[:, :HD] = dq[...]
    out[:, HD:] = acc[...].astype(BF16)


def columns_of(width, height):
    return pl.BlockSpec((height, width), lambda h, *_: (0, h))


def call(kernel, scalars, ins, outs, scratch, heads, flops, name):
    spec = lambda a: columns_of(a.shape[1] // heads, a.shape[0])
    moved = sum(a.size * a.dtype.itemsize for a in (*ins, *outs))
    return pl.pallas_call(
        kernel,
        grid_spec=pltpu.PrefetchScalarGridSpec(
            num_scalar_prefetch=len(scalars),
            grid=(heads,),
            in_specs=[spec(a) for a in ins],
            out_specs=[spec(a) for a in outs],
            scratch_shapes=scratch,
        ),
        out_shape=outs,
        cost_estimate=pl.CostEstimate(flops=flops, bytes_accessed=moved, transcendentals=0),
        name=name,
    )(*scalars, *ins)


def tables(key_lists, live_counts, axes):
    pair_axis, half_axis = axes
    pairs_total = lax.axis_size(pair_axis)
    z = lax.axis_index(pair_axis)
    x = lax.axis_index(half_axis)
    mine = jnp.concatenate([key_lists, live_counts[:, None]], axis=1)
    other = lax.ppermute(mine, half_axis, [(0, 1), (1, 0)])
    pair = jnp.where(x == 0, jnp.concatenate([mine, other]), jnp.concatenate([other, mine]))
    after = lax.ppermute(pair, pair_axis, [(i + 1, i) for i in range(pairs_total - 1)])
    before = lax.ppermute(pair, pair_axis, [(i, i + 1) for i in range(pairs_total - 1)])
    base = z * PAIR
    lists = jnp.stack([after[:TILES], before[TILES:], pair[:TILES], pair[TILES:]])[:, :, :LISTED]
    lists = lists.reshape(4, TILES * LISTED)
    first = base + jnp.array([0, TILES, -PAIR, PAIR + TILES], jnp.int32)
    order = jnp.arange(TILES, dtype=jnp.int32)
    needed = jnp.any(lists[:, :, None] == (first[:, None] + order[None, :])[:, None, :], axis=1)
    earlier = order[None, :] < order[:, None]
    rank = jnp.sum(jnp.where(earlier[None] & needed[:, None, :], 1, 0), axis=2)
    slot = jnp.arange(NAMED, dtype=jnp.int32)
    chosen = needed[:, None, :] & (rank[:, None, :] == slot[None, :, None])
    slots = jnp.sum(jnp.where(chosen, order[None, None, :], 0), axis=2).astype(jnp.int32)[:2]
    rel = pair[:, :LISTED] - base
    pick = lambda table, at: jnp.sum(jnp.where(at[:, :, None] == order, table, 0), axis=2)
    far_left = pick(rank[2], rel + PAIR)
    far_right = EDGE + PAIR + TILES + pick(rank[3], rel - PAIR - TILES)
    places = jnp.where(rel < -TILES, far_left, jnp.where(rel >= PAIR + TILES, far_right, EDGE + rel))
    places = jnp.clip(places, 0, ALL - 1).astype(jnp.int32)
    block = base + jnp.arange(PAIR, dtype=jnp.int32)
    last = pairs_total * PAIR - 1
    info = jnp.stack([pair[:, LISTED], (block > 0).astype(jnp.int32), (block < last).astype(jnp.int32)])
    return slots, places, info


def shards(qkv, grad_out, key_lists, live_counts):
    group = ("cx", "head")
    ways = lax.axis_size("cx") * lax.axis_size("head")
    pairs_total = lax.axis_size("cz")
    up = [(i, i + 1) for i in range(pairs_total - 1)]
    down = [(i + 1, i) for i in range(pairs_total - 1)]
    slots, places, info = tables(key_lists, live_counts, ("cz", "cx"))
    tokens = qkv.shape[0]
    heads = qkv.shape[1] // (3 * HD) // ways // CHUNKS
    split_qkv = qkv.reshape(tokens, ways, CHUNKS, heads * 3 * HD)
    split_grad = grad_out.reshape(tokens, ways, CHUNKS, heads * HD)
    full = tokens * ways
    sds = jax.ShapeDtypeStruct
    edge = sds((EDGE * BLK, heads * 2 * HD), BF16)

    def gathered(part):
        part = lax.all_to_all(part.transpose(1, 0, 2), group, split_axis=0, concat_axis=0, tiled=True)
        return part.reshape(full, part.shape[2])

    owns, gs, lefts, rights = [], [], [], []
    for c in range(CHUNKS):
        own = gathered(split_qkv[:, :, c])
        to_next, to_prev = call(pack_kernel, (slots,), (own,), (edge, edge), [], heads, 0, "pack")
        owns.append(own)
        lefts.append(lax.ppermute(to_next, "cz", up))
        rights.append(lax.ppermute(to_prev, "cz", down))
        gs.append(gathered(split_grad[:, :, c]))
    results = []
    for c in range(CHUNKS):
        outs = (sds((full, heads * HD), BF16), sds((full, heads * 2 * HD), F32), edge, edge)
        scratch = [pltpu.VMEM((ALL * BLK, 2 * HD), BF16), pltpu.VMEM((ALL * BLK, 2 * HD), F32)]
        flops = heads * PAIR * 5 * 2 * BLK * 7 * BLK * HD
        dq, own_grads, left_grads, right_grads = call(
            attention_kernel, (places, info), (owns[c], gs[c], lefts[c], rights[c]), outs, scratch, heads, flops, "attention"
        )
        from_next = lax.ppermute(left_grads, "cz", down)
        from_prev = lax.ppermute(right_grads, "cz", up)
        (joined,) = call(
            combine_kernel, (slots,), (dq, own_grads, from_next, from_prev), (sds((full, heads * 3 * HD), BF16),),
            [pltpu.VMEM((PAIR * BLK, 2 * HD), F32)], heads, 0, "combine",
        )
        joined = joined.reshape(ways, tokens, heads * 3 * HD)
        results.append(lax.all_to_all(joined, group, split_axis=0, concat_axis=0, tiled=True))
    return jnp.stack(results, axis=1).transpose(2, 0, 1, 3).reshape(qkv.shape)


def solution(mesh):
    ctx, head = mesh.shape["ctx"], mesh.shape["head"]
    split = Mesh(mesh.devices.reshape(ctx // 2, 2, head), ("cz", "cx", "head"))
    both = ("cz", "cx")
    tokens = P((*both, "head"), None)
    return jax.shard_map(
        shards, mesh=split, in_specs=(tokens, tokens, P(both, None), P(both)), out_specs=tokens, check_vma=False
    )
```

time: 681 us -> 234 us (0.34); the launches traced: 669 us -> 233 us
  local copies, waits for them, and re-layouts: 318 us -> 35.3 us
  matrix products: 83.8 us -> 0 us
  starting transfers between devices: 111 us -> 49.6 us
  Pallas kernels: 0 us -> 60.4 us
  other arithmetic: 38.5 us -> 3.03 us
  waiting for transfers between devices: 76.7 us -> 60.3 us
  blocking collectives: 39.4 us -> 23.8 us
    dot_general x21 -> x0, matrix products: 74.9 us -> none  [the longest x4 28 us: shards(): jnp.einsum('st,sbf->tbf', owner_tables[side_index], arrived, precision=la...]
    ppermute x16 -> x11, starting transfers between devices: 103 us -> 29.9 us  [the longest x2 10 us: shards(): from_prev = lax.ppermute(right_grads, 'cz', up)]
    reshape x5 -> x3, local copies, waits for them, and re-layouts: 73.6 us -> 12.4 us  [the longest x1 7.07 us: shards(): split_qkv = qkv.reshape(tokens, ways, CHUNKS, heads * 3 * HD)]
    pallas_call x0 -> x6, Pallas kernels: none -> 60.4 us  [call(): pl.pallas_call(kernel, grid_spec=pltpu.PrefetchScalarGridSpec(num_scalar_...]
    dynamic_update_slice x4 -> x0, local copies, waits for them, and re-layouts: 46.9 us -> none  [shards(): lax.scan(step, carry_zero, (query_blocks, grad_blocks, places, usable))]
    slice x14 -> x3, local copies, waits for them, and re-layouts: 50 us -> 8.53 us  [the longest x1 6.05 us: shards(): own = gathered(split_qkv[:, :, c])]
    scatter-add x2 -> x0, local copies, waits for them, and re-layouts: 39.4 us -> none  [shards(): own_grads = own_grads.at[target_block].add(arrived)]
    gather x4 -> x0, local copies, waits for them, and re-layouts: 24.2 us -> none  [step(): chosen = tile_ordinals[block_places]]
  transfers between devices with their start and end apart: 18 -> 16, of which waited for: 4 -> 10; matrix products, arithmetic and copies ran while one was open for 28% -> 12% of each run, Pallas kernels for 0% -> 26%
where the time goes in v1:
time: 234 us; the launch traced here: 233 us
  Pallas kernels  60.4 us (26%)
  waiting for transfers between devices  60.3 us (26%)
  starting transfers between devices  49.6 us (21%)
  local copies, waits for them, and re-layouts  35.3 us (15%)
  blocking collectives  23.8 us (10%)
  other arithmetic  3.03 us (1%)
    pallas_call x6, Pallas kernels, call(): pl.pallas_call(kernel, grid_spec=pltpu.PrefetchScalarGridSpec(num_scalar_...  60.4 us
    all_to_all x1, blocking collectives, shards(): lax.all_to_all(joined, group, split_axis=0, concat_axis=0, tiled=True)  23.8 us
    ppermute x2, waiting for transfers between devices, shards(): lefts.append(lax.ppermute(to_next, 'cz', up))  21.6 us
    ppermute x2, waiting for transfers between devices, shards(): from_next = lax.ppermute(left_grads, 'cz', down)  16.2 us
    all_to_all x4, starting transfers between devices, gathered(): lax.all_to_all(part.transpose(1, 0, 2), group, split_axis=0, concat_axis=...  15.9 us
    ppermute x2, starting transfers between devices, shards(): from_prev = lax.ppermute(right_grads, 'cz', up)  10 us
    unnamed x25, local copies, waits for them, and re-layouts  9.9 us
    all_to_all x4, waiting for transfers between devices, gathered(): lax.all_to_all(part.transpose(1, 0, 2), group, split_axis=0, concat_axis=...  8.52 us
  transfers between devices with their start and end apart: 16, of which 10 were waited for; matrix products, arithmetic and copies ran while one was open for 12% of the time, Pallas kernels for 26%

profile of v1, /device:TPU:0, one launch (start us, length us, event | category | flops | bytes accessed | tf_op | source)
XLA Modules:
  0.0 232.6 jit_solution(15546222464347092087)
XLA Ops:
  1.5 3.0 %collective-permute-start = (s32[4,5]{1,0:T(4,128)S(1)}, s32[4,5]{1,0:T(4,128)S(1)}, u32[]{:S(2)}, u32[]{:S(2)}) collective-permute-start(s32[4,5]{1,0:T(4,128)S(1)} %pad_add_fusion.3), channel_id=1, source_target_pairs={{0,4},{4,0},{1,5},{5,1},{2,6},{6,2},{3,7},{7,3},{8,12},{12,8},{9,1... | collective-permute-start | bytes 248 | tf_op jit(solution)/shard_map/ppermute | solution.py:121
  6.3 2.3 fusion.4
  9.7 4.1 %all-to-all-start.4 = ((bf16[8,128,256]{2,1,0:T(8,128)(2,1)}), bf16[8,128,256]{2,1,0:T(8,128)(2,1)}, u32[]{:S(2)}, u32[]{:S(2)}) async-start(bf16[8,128,256]{2,1,0:T(8,128)(2,1)} %bitcast.42), calls=%async_computation.4 | async-start | bytes 1048576 | tf_op jit(solution)/shard_map/all_to_all | solution.py:164
  13.8 7.1 %reshape.81 = bf16[128,8,2,768]{3,2,1,0:T(2,128)(2,1)S(1)} reshape(bf16[128,12288]{1,0:T(8,128)(2,1)} %param.5) | data formatting | bytes 6291456 | tf_op jit(solution)/shard_map/reshape | solution.py:157
  20.9 6.0 %fusion.3 = (bf16[128,8,1,768]{3,2,1,0:T(2,128)(2,1)}, bf16[128,8,1,768]{3,2,1,0:T(2,128)(2,1)}) fusion(bf16[128,8,2,768]{3,2,1,0:T(2,128)(2,1)S(1)} %reshape.81), kind=kLoop, calls=%fused_computation.37 | loop fusion | bytes 6291456 | tf_op jit(solution)/shard_map/slice | solution.py:169
  27.0 4.1 %copy.38 = bf16[128,8,1,768]{3,0,1,2:T(8,128)(2,1)} copy(bf16[128,8,1,768]{3,2,1,0:T(2,128)(2,1)} %get-tuple-element.30) | data formatting | bytes 3145728
  31.2 4.3 %all-to-all-start.3 = ((bf16[8,128,768]{2,1,0:T(8,128)(2,1)}), bf16[8,128,768]{2,1,0:T(8,128)(2,1)}, u32[]{:S(2)}, u32[]{:S(2)}) async-start(bf16[8,128,768]{2,1,0:T(8,128)(2,1)} %bitcast.48), calls=%async_computation.3 | async-start | bytes 3145728 | tf_op jit(solution)/shard_map/all_to_all | solution.py:164
  35.5 2.0 copy.39
  37.6 3.5 %collective-permute-start.2 = (s32[8,5]{1,0:T(8,128)S(1)}, s32[8,5]{1,0:T(8,128)S(1)}, u32[]{:S(2)}, u32[]{:S(2)}) collective-permute-start(s32[8,5]{1,0:T(8,128)S(1)} %add_select_fusion), channel_id=1, source_target_pairs={{0,8},{8,16},{16,24},{1,9},{9,17},{17,25},{2,10},{10,18},{18,26},{... | collective-permute-start | bytes 488 | tf_op jit(solution)/shard_map/ppermute | solution.py:124
  42.6 4.0 %collective-permute-done.1 = s32[8,5]{1,0:T(8,128)S(1)} collective-permute-done((s32[8,5]{1,0:T(8,128)S(1)}, s32[8,5]{1,0:T(8,128)S(1)}, u32[]{:S(2)}, u32[]{:S(2)}) %collective-permute-start.1) | collective-permute-done | bytes 192 | tf_op jit(solution)/shard_map/ppermute | solution.py:123
  47.1 8.5 %all-to-all-done.3 = bf16[8,128,768]{2,1,0:T(8,128)(2,1)} async-done(((bf16[8,128,768]{2,1,0:T(8,128)(2,1)}), bf16[8,128,768]{2,1,0:T(8,128)(2,1)}, u32[]{:S(2)}, u32[]{:S(2)}) %all-to-all-start.3) | async-done | bytes 1572896 | tf_op jit(solution)/shard_map/all_to_all | solution.py:164
  55.6 3.6 %all-to-all-start = ((bf16[8,128,768]{2,1,0:T(8,128)(2,1)}), bf16[8,128,768]{2,1,0:T(8,128)(2,1)S(1)}, u32[]{:S(2)}, u32[]{:S(2)}) async-start(bf16[8,128,768]{2,1,0:T(8,128)(2,1)} %bitcast.47), calls=%async_computation | async-start | bytes 3145728 | tf_op jit(solution)/shard_map/all_to_all | solution.py:164
  59.9 3.1 %pack.3 = (bf16[768,512]{1,0:T(8,128)(2,1)}, bf16[768,512]{1,0:T(8,128)(2,1)}) custom-call(s32[2,2]{1,0:T(2,128)} %copy.29.slots, bf16[1024,768]{1,0:T(8,128)(2,1)} %bitcast.17.own), custom_call_target="tpu_custom_call" | custom-call | bytes 3145728 | tf_op jit(solution)/shard_map/pack/pallas_call | solution.py:100
  63.0 3.5 %collective-permute-start.7 = (bf16[768,512]{1,0:T(8,128)(2,1)}, bf16[768,512]{1,0:T(8,128)(2,1)S(1)}, u32[]{:S(2)}, u32[]{:S(2)}) collective-permute-start(bf16[768,512]{1,0:T(8,128)(2,1)} %get-tuple-element.23), channel_id=1, source_target_pairs={{0,8},{8,16},{16,24},{1,9},{9,17},{17,25},{2,10},{10,18},{18,26},{... | collective-permute-start | bytes 2359304 | tf_op jit(solution)/shard_map/ppermute | solution.py:172
  69.5 14.7 %collective-permute-done.7.left = bf16[768,512]{1,0:T(8,128)(2,1)S(1)} collective-permute-done((bf16[768,512]{1,0:T(8,128)(2,1)}, bf16[768,512]{1,0:T(8,128)(2,1)S(1)}, u32[]{:S(2)}, u32[]{:S(2)}) %collective-permute-start.7) | collective-permute-done | bytes 786464 | tf_op jit(solution)/shard_map/ppermute | solution.py:172
  84.1 4.2 %collective-permute-done.8.right = bf16[768,512]{1,0:T(8,128)(2,1)} collective-permute-done((bf16[768,512]{1,0:T(8,128)(2,1)}, bf16[768,512]{1,0:T(8,128)(2,1)}, u32[]{:S(2)}, u32[]{:S(2)}) %collective-permute-start.8) | collective-permute-done | bytes 786464 | tf_op jit(solution)/shard_map/ppermute | solution.py:173
  88.3 23.1 %attention.3 = (bf16[1024,256]{1,0:T(8,128)(2,1)}, f32[1024,512]{1,0:T(8,128)}, bf16[768,512]{1,0:T(8,128)(2,1)}, bf16[768,512]{1,0:T(8,128)(2,1)}) custom-call(s32[8,4]{1,0:T(8,128)} %select_clamp_fusion.places, s32[3,8]{1,0:T(4,128)} %pad_add_fusion.4.info, bf16[1024,768]{1,0:T(8,128)(2,1)} %bitcast.17.own, bf16[1024,256]{1,0:T(8,128)(2,1)} %bitcast.20.grads, ...), custom_call_target="tpu_custom_call" | custom-call | flops 2348810240 | bytes 7864320 | tf_op jit(solution)/shard_map/attention/pallas_call | solution.py:100
  112.7 5.4 %collective-permute-start.10 = (bf16[768,512]{1,0:T(8,128)(2,1)}, bf16[768,512]{1,0:T(8,128)(2,1)}, u32[]{:S(2)}, u32[]{:S(2)}) collective-permute-start(bf16[768,512]{1,0:T(8,128)(2,1)} %get-tuple-element.28), channel_id=1, source_target_pairs={{0,8},{8,16},{16,24},{1,9},{9,17},{17,25},{2,10},{10,18},{18,26},{... | collective-permute-start | bytes 2359304 | tf_op jit(solution)/shard_map/ppermute | solution.py:184
  119.3 3.8 %all-to-all-start.1 = ((bf16[8,128,256]{2,1,0:T(8,128)(2,1)}), bf16[8,128,256]{2,1,0:T(8,128)(2,1)S(1)}, u32[]{:S(2)}, u32[]{:S(2)}) async-start(bf16[8,128,256]{2,1,0:T(8,128)(2,1)} %bitcast.43), calls=%async_computation.1 | async-start | bytes 1048576 | tf_op jit(solution)/shard_map/all_to_all | solution.py:164
  123.2 3.1 %pack.2 = (bf16[768,512]{1,0:T(8,128)(2,1)}, bf16[768,512]{1,0:T(8,128)(2,1)}) custom-call(s32[2,2]{1,0:T(2,128)} %copy.29.slots, bf16[1024,768]{1,0:T(8,128)(2,1)} %bitcast.45), custom_call_target="tpu_custom_call" | custom-call | bytes 3145728 | tf_op jit(solution)/shard_map/pack/pallas_call | solution.py:100
  126.2 3.5 %collective-permute-start.3 = (bf16[768,512]{1,0:T(8,128)(2,1)}, bf16[768,512]{1,0:T(8,128)(2,1)}, u32[]{:S(2)}, u32[]{:S(2)}) collective-permute-start(bf16[768,512]{1,0:T(8,128)(2,1)} %get-tuple-element.17), channel_id=1, source_target_pairs={{0,8},{8,16},{16,24},{1,9},{9,17},{17,25},{2,10},{10,18},{18,26},{... | collective-permute-start | bytes 2359304 | tf_op jit(solution)/shard_map/ppermute | solution.py:172
  132.2 3.3 %collective-permute-done.10.from_prev = bf16[768,512]{1,0:T(8,128)(2,1)} collective-permute-done((bf16[768,512]{1,0:T(8,128)(2,1)}, bf16[768,512]{1,0:T(8,128)(2,1)}, u32[]{:S(2)}, u32[]{:S(2)}) %collective-permute-start.10) | collective-permute-done | bytes 786464 | tf_op jit(solution)/shard_map/ppermute | solution.py:184
  135.5 4.1 %combine.3 = bf16[1024,768]{1,0:T(8,128)(2,1)} custom-call(s32[2,2]{1,0:T(2,128)} %copy.29.slots, bf16[1024,256]{1,0:T(8,128)(2,1)} %get-tuple-element.25.dq, f32[1024,512]{1,0:T(8,128)} %get-tuple-element.26.own_grads, bf16[768,512]{1,0:T(8,128)(2,1)} %copy-done.3, bf16[768,512]{1,0:T(8,128)(2,1)} %collective-permute-done.10.from_prev), custom_call_target="tpu_custom_call" | custom-call | bytes 5767168 | tf_op jit(solution)/shard_map/combine/pallas_call | solution.py:100
  139.6 3.9 %all-to-all-start.5 = ((bf16[8,128,768]{2,1,0:T(8,128)(2,1)}), bf16[8,128,768]{2,1,0:T(8,128)(2,1)S(1)}, u32[]{:S(2)}, u32[]{:S(2)}) async-start(bf16[8,128,768]{2,1,0:T(8,128)(2,1)} %bitcast.49), calls=%async_computation.5 | async-start | bytes 3145728 | tf_op jit(solution)/shard_map/all_to_all | solution.py:190
  143.4 6.9 %collective-permute-done.3.left = bf16[768,512]{1,0:T(8,128)(2,1)} collective-permute-done((bf16[768,512]{1,0:T(8,128)(2,1)}, bf16[768,512]{1,0:T(8,128)(2,1)}, u32[]{:S(2)}, u32[]{:S(2)}) %collective-permute-start.3) | collective-permute-done | bytes 786464 | tf_op jit(solution)/shard_map/ppermute | solution.py:172
  151.6 23.0 %attention.2 = (bf16[1024,256]{1,0:T(8,128)(2,1)}, f32[1024,512]{1,0:T(8,128)}, bf16[768,512]{1,0:T(8,128)(2,1)}, bf16[768,512]{1,0:T(8,128)(2,1)}) custom-call(s32[8,4]{1,0:T(8,128)} %select_clamp_fusion.places, s32[3,8]{1,0:T(4,128)} %pad_add_fusion.4.info, bf16[1024,768]{1,0:T(8,128)(2,1)} %bitcast.46, bf16[1024,256]{1,0:T(8,128)(2,1)} %bitcast.53, ...), custom_call_target="tpu_custom_call" | custom-call | flops 2348810240 | bytes 7864320 | tf_op jit(solution)/shard_map/attention/pallas_call | solution.py:100
  175.9 4.6 %collective-permute-start.6 = (bf16[768,512]{1,0:T(8,128)(2,1)}, bf16[768,512]{1,0:T(8,128)(2,1)S(1)}, u32[]{:S(2)}, u32[]{:S(2)}) collective-permute-start(bf16[768,512]{1,0:T(8,128)(2,1)} %get-tuple-element.22), channel_id=1, source_target_pairs={{0,8},{8,16},{16,24},{1,9},{9,17},{17,25},{2,10},{10,18},{18,26},{... | collective-permute-start | bytes 2359304 | tf_op jit(solution)/shard_map/ppermute | solution.py:184
  180.5 15.0 %collective-permute-done.5.from_next = bf16[768,512]{1,0:T(8,128)(2,1)S(1)} collective-permute-done((bf16[768,512]{1,0:T(8,128)(2,1)}, bf16[768,512]{1,0:T(8,128)(2,1)S(1)}, u32[]{:S(2)}, u32[]{:S(2)}) %collective-permute-start.5) | collective-permute-done | bytes 786464 | tf_op jit(solution)/shard_map/ppermute | solution.py:183
  197.6 4.1 %combine.2 = bf16[1024,768]{1,0:T(8,128)(2,1)} custom-call(s32[2,2]{1,0:T(2,128)} %copy.29.slots, bf16[1024,256]{1,0:T(8,128)(2,1)} %get-tuple-element.19.dq, f32[1024,512]{1,0:T(8,128)} %get-tuple-element.20.own_grads, bf16[768,512]{1,0:T(8,128)(2,1)} %copy-done.4, bf16[768,512]{1,0:T(8,128)(2,1)} %copy-done.5), custom_call_target="tpu_custom_call" | custom-call | bytes 5767168 | tf_op jit(solution)/shard_map/combine/pallas_call | solution.py:100
  201.7 23.8 %all_to_all.30 = bf16[8,128,768]{2,1,0:T(8,128)(2,1)S(1)} all-to-all(bf16[8,128,768]{2,1,0:T(8,128)(2,1)} %bitcast.51), channel_id=1, replica_groups=mesh['cz'=4,'cx'=2,'head'=4] {'cx','head'}, dimensions={0} | all-to-all | bytes 3145728 | tf_op jit(solution)/shard_map/all_to_all | solution.py:190
  225.8 3.2 %copy.28 = bf16[128,8,2,768]{3,2,1,0:T(2,128)(2,1)S(1)} copy(bf16[128,8,2,768]{3,0,1,2:T(8,128)(2,1)S(1)} %maximum_bitcast_fusion) | data formatting | bytes 6291456 | tf_op jit(solution)/shard_map/transpose | solution.py:191
  229.1 3.5 %reshape.89 = bf16[128,12288]{1,0:T(8,128)(2,1)} reshape(bf16[128,8,2,768]{3,2,1,0:T(2,128)(2,1)S(1)} %copy.28) | data formatting | bytes 6291456 | tf_op jit(solution)/shard_map/reshape | solution.py:191
  (64 shorter events, 20.1 us)
Async XLA Ops:
  1.5 36.0 %collective-permute-start = (s32[4,5]{1,0:T(4,128)S(1)}, s32[4,5]{1,0:T(4,128)S(1)}, u32[]{:S(2)}, u32[]{:S(2)}) collective-permute-start(s32[4,5]{1,0:T(4,128)S(1)} %pad_add_fusion.3), channel_id=1, source_target_pairs={{0,4},{4,0},{1,5},{5,1},{2,6},{6,2},{3,7},{7,3},{8,12},{12,8},{9,1... | collective-permute-start | bytes 248 | tf_op jit(solution)/shard_map/ppermute | solution.py:121
  9.7 21.5 %all-to-all-start.4 = ((bf16[8,128,256]{2,1,0:T(8,128)(2,1)}), bf16[8,128,256]{2,1,0:T(8,128)(2,1)}, u32[]{:S(2)}, u32[]{:S(2)}) async-start(bf16[8,128,256]{2,1,0:T(8,128)(2,1)} %bitcast.42), calls=%async_computation.4 | async-start | bytes 1048576 | tf_op jit(solution)/shard_map/all_to_all | solution.py:164
  27.0 4.1 %copy-start.9 = (s32[4]{0:T(128)S(1)}, s32[4]{0:T(128)}, u32[]{:S(2)}) copy-start(s32[4]{0:T(128)} %constant.39.clone) | copy-start | bytes 52
  27.0 8.5 %copy-start = (bf16[128,8,1,768]{3,2,1,0:T(2,128)(2,1)S(1)}, bf16[128,8,1,768]{3,2,1,0:T(2,128)(2,1)}, u32[]{:S(2)}) copy-start(bf16[128,8,1,768]{3,2,1,0:T(2,128)(2,1)} %get-tuple-element.29) | copy-start | bytes 4718596
  31.2 24.4 %all-to-all-start.3 = ((bf16[8,128,768]{2,1,0:T(8,128)(2,1)}), bf16[8,128,768]{2,1,0:T(8,128)(2,1)}, u32[]{:S(2)}, u32[]{:S(2)}) async-start(bf16[8,128,768]{2,1,0:T(8,128)(2,1)} %bitcast.48), calls=%async_computation.3 | async-start | bytes 3145728 | tf_op jit(solution)/shard_map/all_to_all | solution.py:164
  35.5 2.1 copy-start.7
  37.6 5.0 %collective-permute-start.2 = (s32[8,5]{1,0:T(8,128)S(1)}, s32[8,5]{1,0:T(8,128)S(1)}, u32[]{:S(2)}, u32[]{:S(2)}) collective-permute-start(s32[8,5]{1,0:T(8,128)S(1)} %add_select_fusion), channel_id=1, source_target_pairs={{0,8},{8,16},{16,24},{1,9},{9,17},{17,25},{2,10},{10,18},{18,26},{... | collective-permute-start | bytes 488 | tf_op jit(solution)/shard_map/ppermute | solution.py:124
  41.1 5.5 %collective-permute-start.1 = (s32[8,5]{1,0:T(8,128)S(1)}, s32[8,5]{1,0:T(8,128)S(1)}, u32[]{:S(2)}, u32[]{:S(2)}) collective-permute-start(s32[8,5]{1,0:T(8,128)S(1)} %add_select_fusion), channel_id=1, source_target_pairs={{8,0},{16,8},{24,16},{9,1},{17,9},{25,17},{10,2},{18,10},{26,18},{... | collective-permute-start | bytes 488 | tf_op jit(solution)/shard_map/ppermute | solution.py:123
  55.6 63.7 %all-to-all-start = ((bf16[8,128,768]{2,1,0:T(8,128)(2,1)}), bf16[8,128,768]{2,1,0:T(8,128)(2,1)S(1)}, u32[]{:S(2)}, u32[]{:S(2)}) async-start(bf16[8,128,768]{2,1,0:T(8,128)(2,1)} %bitcast.47), calls=%async_computation | async-start | bytes 3145728 | tf_op jit(solution)/shard_map/all_to_all | solution.py:164
  63.0 21.1 %collective-permute-start.7 = (bf16[768,512]{1,0:T(8,128)(2,1)}, bf16[768,512]{1,0:T(8,128)(2,1)S(1)}, u32[]{:S(2)}, u32[]{:S(2)}) collective-permute-start(bf16[768,512]{1,0:T(8,128)(2,1)} %get-tuple-element.23), channel_id=1, source_target_pairs={{0,8},{8,16},{16,24},{1,9},{9,17},{17,25},{2,10},{10,18},{18,26},{... | collective-permute-start | bytes 2359304 | tf_op jit(solution)/shard_map/ppermute | solution.py:172
  66.5 21.8 %collective-permute-start.8 = (bf16[768,512]{1,0:T(8,128)(2,1)}, bf16[768,512]{1,0:T(8,128)(2,1)}, u32[]{:S(2)}, u32[]{:S(2)}) collective-permute-start(bf16[768,512]{1,0:T(8,128)(2,1)} %get-tuple-element.24), channel_id=1, source_target_pairs={{8,0},{16,8},{24,16},{9,1},{17,9},{25,17},{10,2},{18,10},{26,18},{... | collective-permute-start | bytes 2359304 | tf_op jit(solution)/shard_map/ppermute | solution.py:173
  84.1 4.2 %copy-start.8 = (bf16[768,512]{1,0:T(8,128)(2,1)}, bf16[768,512]{1,0:T(8,128)(2,1)S(1)}, u32[]{:S(2)}) copy-start(bf16[768,512]{1,0:T(8,128)(2,1)S(1)} %collective-permute-done.7.left) | copy-start | bytes 2359300
  88.3 29.9 %copy-start.2 = (bf16[128,8,1,256]{3,2,1,0:T(2,128)(2,1)S(1)}, bf16[128,8,1,256]{3,2,1,0:T(2,128)(2,1)}, u32[]{:S(2)}) copy-start(bf16[128,8,1,256]{3,2,1,0:T(2,128)(2,1)} %get-tuple-element.31) | copy-start | bytes 1572868
  111.4 20.8 %collective-permute-start.9 = (bf16[768,512]{1,0:T(8,128)(2,1)}, bf16[768,512]{1,0:T(8,128)(2,1)S(1)}, u32[]{:S(2)}, u32[]{:S(2)}) collective-permute-start(bf16[768,512]{1,0:T(8,128)(2,1)} %get-tuple-element.27), channel_id=1, source_target_pairs={{8,0},{16,8},{24,16},{9,1},{17,9},{25,17},{10,2},{18,10},{26,18},{... | collective-permute-start | bytes 2359304 | tf_op jit(solution)/shard_map/ppermute | solution.py:183
  112.7 22.8 %collective-permute-start.10 = (bf16[768,512]{1,0:T(8,128)(2,1)}, bf16[768,512]{1,0:T(8,128)(2,1)}, u32[]{:S(2)}, u32[]{:S(2)}) collective-permute-start(bf16[768,512]{1,0:T(8,128)(2,1)} %get-tuple-element.28), channel_id=1, source_target_pairs={{0,8},{8,16},{16,24},{1,9},{9,17},{17,25},{2,10},{10,18},{18,26},{... | collective-permute-start | bytes 2359304 | tf_op jit(solution)/shard_map/ppermute | solution.py:184
  119.3 3.9 %copy-start.1 = (bf16[8,128,768]{2,1,0:T(8,128)(2,1)}, bf16[8,128,768]{2,1,0:T(8,128)(2,1)S(1)}, u32[]{:S(2)}) copy-start(bf16[8,128,768]{2,1,0:T(8,128)(2,1)S(1)} %all-to-all-done) | copy-start | bytes 4718596
  119.3 20.3 %all-to-all-start.1 = ((bf16[8,128,256]{2,1,0:T(8,128)(2,1)}), bf16[8,128,256]{2,1,0:T(8,128)(2,1)S(1)}, u32[]{:S(2)}, u32[]{:S(2)}) async-start(bf16[8,128,256]{2,1,0:T(8,128)(2,1)} %bitcast.43), calls=%async_computation.1 | async-start | bytes 1048576 | tf_op jit(solution)/shard_map/all_to_all | solution.py:164
  126.2 24.1 %collective-permute-start.3 = (bf16[768,512]{1,0:T(8,128)(2,1)}, bf16[768,512]{1,0:T(8,128)(2,1)}, u32[]{:S(2)}, u32[]{:S(2)}) collective-permute-start(bf16[768,512]{1,0:T(8,128)(2,1)} %get-tuple-element.17), channel_id=1, source_target_pairs={{0,8},{8,16},{16,24},{1,9},{9,17},{17,25},{2,10},{10,18},{18,26},{... | collective-permute-start | bytes 2359304 | tf_op jit(solution)/shard_map/ppermute | solution.py:172
  129.7 21.9 %collective-permute-start.4 = (bf16[768,512]{1,0:T(8,128)(2,1)}, bf16[768,512]{1,0:T(8,128)(2,1)}, u32[]{:S(2)}, u32[]{:S(2)}) collective-permute-start(bf16[768,512]{1,0:T(8,128)(2,1)} %get-tuple-element.18), channel_id=1, source_target_pairs={{8,0},{16,8},{24,16},{9,1},{17,9},{25,17},{10,2},{18,10},{26,18},{... | collective-permute-start | bytes 2359304 | tf_op jit(solution)/shard_map/ppermute | solution.py:173
  132.2 3.3 %copy-start.3 = (bf16[768,512]{1,0:T(8,128)(2,1)}, bf16[768,512]{1,0:T(8,128)(2,1)S(1)}, u32[]{:S(2)}) copy-start(bf16[768,512]{1,0:T(8,128)(2,1)S(1)} %collective-permute-done.9.from_next) | copy-start | bytes 2359300
  139.6 12.0 %copy-start.6 = (bf16[8,128,256]{2,1,0:T(8,128)(2,1)}, bf16[8,128,256]{2,1,0:T(8,128)(2,1)S(1)}, u32[]{:S(2)}) copy-start(bf16[8,128,256]{2,1,0:T(8,128)(2,1)S(1)} %all-to-all-done.1) | copy-start | bytes 1572868
  139.6 62.2 %all-to-all-start.5 = ((bf16[8,128,768]{2,1,0:T(8,128)(2,1)}), bf16[8,128,768]{2,1,0:T(8,128)(2,1)S(1)}, u32[]{:S(2)}, u32[]{:S(2)}) async-start(bf16[8,128,768]{2,1,0:T(8,128)(2,1)} %bitcast.49), calls=%async_computation.5 | async-start | bytes 3145728 | tf_op jit(solution)/shard_map/all_to_all | solution.py:190
  174.6 20.9 %collective-permute-start.5 = (bf16[768,512]{1,0:T(8,128)(2,1)}, bf16[768,512]{1,0:T(8,128)(2,1)S(1)}, u32[]{:S(2)}, u32[]{:S(2)}) collective-permute-start(bf16[768,512]{1,0:T(8,128)(2,1)} %get-tuple-element.21), channel_id=1, source_target_pairs={{8,0},{16,8},{24,16},{9,1},{17,9},{25,17},{10,2},{18,10},{26,18},{... | collective-permute-start | bytes 2359304 | tf_op jit(solution)/shard_map/ppermute | solution.py:183
  175.9 20.9 %collective-permute-start.6 = (bf16[768,512]{1,0:T(8,128)(2,1)}, bf16[768,512]{1,0:T(8,128)(2,1)S(1)}, u32[]{:S(2)}, u32[]{:S(2)}) collective-permute-start(bf16[768,512]{1,0:T(8,128)(2,1)} %get-tuple-element.22), channel_id=1, source_target_pairs={{0,8},{8,16},{16,24},{1,9},{9,17},{17,25},{2,10},{10,18},{18,26},{... | collective-permute-start | bytes 2359304 | tf_op jit(solution)/shard_map/ppermute | solution.py:184
  195.5 1.3 copy-start.4
  196.8 0.9 copy-start.5

commit v2 on v1

v2 whole, which is shorter than its diff:
```python
import functools

import jax
import jax.numpy as jnp
from jax import lax
from jax.experimental import pallas as pl
from jax.experimental.pallas import tpu as pltpu
from jax.sharding import Mesh, PartitionSpec as P

HD = 128
BLK = 128
TILES = 4
LISTED = 4
NAMED = 2
PAIR = 2 * TILES
EDGE = NAMED + TILES
ALL = 2 * EDGE + PAIR
SCALE = HD ** (-0.5)
MESH = pl.DeviceIdType.MESH
TOGETHER = 2
F32 = jnp.float32
BF16 = jnp.bfloat16


def rows(block, count=1):
    start = block * BLK
    return pl.ds(start if isinstance(start, int) else pl.multiple_of(start, BLK), count * BLK)


def position(sizes):
    pairs_total, heads_total, ways = sizes
    z = lax.axis_index("cz")
    me = lax.axis_index("cx") * heads_total + lax.axis_index("head")
    return z, me


def peer_id(peer, sizes):
    return {"cx": peer // sizes[1], "head": peer % sizes[1]}


def greet(sizes):
    pairs_total, _, ways = sizes
    z, me = position(sizes)
    barrier = pltpu.get_barrier_semaphore()

    def signal(device_id):
        pl.semaphore_signal(barrier, inc=1, device_id=device_id, device_id_type=MESH)

    for k in range(1, ways):
        signal(peer_id((me + k) % ways, sizes))
    pl.when(z > 0)(lambda: signal({"cz": z - 1}))
    pl.when(z < pairs_total - 1)(lambda: signal({"cz": z + 1}))
    pl.semaphore_wait(barrier, ways - 1 + jnp.minimum(z, 1) + jnp.minimum(pairs_total - 1 - z, 1))


def remote(src, dst, send, recv, device_id):
    return pltpu.make_async_remote_copy(
        src_ref=src, dst_ref=dst, send_sem=send, recv_sem=recv, device_id=device_id, device_id_type=MESH
    )


def gather_kernel(sizes, slots, qkv, grads, own, left, right, stage, send, recv, local, edge_send, edge_recv):
    pairs_total, _, ways = sizes
    heads = own.shape[0]
    z, me = position(sizes)
    wide, slim = 3 * HD, HD
    greet(sizes)

    def pieces(h, device, block):
        at = device * heads + h
        return (
            (qkv.at[:, pl.ds(pl.multiple_of(at * wide, HD), wide)], own.at[h, rows(block), pl.ds(0, wide)]),
            (grads.at[:, pl.ds(pl.multiple_of(at * slim, HD), slim)], own.at[h, rows(block), pl.ds(wide, slim)]),
        )

    sends, locals_ = [], []
    for h in range(heads):
        for k in range(1, ways):
            peer = (me + k) % ways
            for t, (src, dst) in enumerate(pieces(h, peer, me)):
                copy = remote(src, dst, send.at[h, k, t], recv.at[h, k, t], peer_id(peer, sizes))
                copy.start()
                sends.append(copy)
        for t, (src, dst) in enumerate(pieces(h, me, me)):
            copy = pltpu.make_async_copy(src, dst, local.at[h, t])
            copy.start()
            locals_.append(copy)

    @pl.when(z == 0)
    def _():
        left[...] = jnp.zeros_like(left)

    @pl.when(z == pairs_total - 1)
    def _():
        right[...] = jnp.zeros_like(right)

    kv = pl.ds(HD, 2 * HD)

    def edge_copies(h):
        up = [
            remote(src, left.at[h, part], edge_send.at[h, 0, n], edge_recv.at[h, 0, n], {"cz": z + 1})
            for n, (src, part) in enumerate(
                ((stage.at[h, 0], rows(0, NAMED)), (own.at[h, rows(TILES, TILES), kv], rows(NAMED, TILES)))
            )
        ]
        down = [
            remote(src, right.at[h, part], edge_send.at[h, 1, n], edge_recv.at[h, 1, n], {"cz": z - 1})
            for n, (src, part) in enumerate(
                ((stage.at[h, 1], rows(TILES, NAMED)), (own.at[h, rows(0, TILES), kv], rows(0, TILES)))
            )
        ]
        return up, down

    for h in range(heads):
        for k in range(1, ways):
            source = (me + ways - k) % ways
            for t, (src, dst) in enumerate(pieces(h, source, source)):
                remote(src, dst, send.at[h, k, t], recv.at[h, k, t], peer_id(source, sizes)).wait_recv()
        locals_[2 * h].wait()
        locals_[2 * h + 1].wait()
        for s in range(NAMED):
            for side in range(2):
                chosen = own[h, rows(side * TILES), HD : 3 * HD]
                for t in range(1, TILES):
                    chosen = jnp.where(slots[side, s] == t, own[h, rows(side * TILES + t), HD : 3 * HD], chosen)
                stage[h, side, rows(s), :] = chosen
        up, down = edge_copies(h)
        pl.when(z < pairs_total - 1)(lambda: [c.start() for c in up] and None)
        pl.when(z > 0)(lambda: [c.start() for c in down] and None)
    for h in range(heads):
        up, down = edge_copies(h)
        pl.when(z > 0)(lambda: [c.wait_recv() for c in up] and None)
        pl.when(z < pairs_total - 1)(lambda: [c.wait_recv() for c in down] and None)
        pl.when(z < pairs_total - 1)(lambda: [c.wait_send() for c in up] and None)
        pl.when(z > 0)(lambda: [c.wait_send() for c in down] and None)
    for copy in sends:
        copy.wait_send()


def return_kernel(
    sizes, slots, dq, own_grads, left_grads, right_grads, out,
    from_next, from_prev, joined, send, recv, local, edge_send, edge_recv,
):
    pairs_total, _, ways = sizes
    heads = dq.shape[0]
    z, me = position(sizes)
    wide = 3 * HD
    greet(sizes)

    @pl.when(z == 0)
    def _():
        from_prev[...] = jnp.zeros_like(from_prev)

    @pl.when(z == pairs_total - 1)
    def _():
        from_next[...] = jnp.zeros_like(from_next)

    def edge_copies(h):
        return (
            remote(right_grads.at[h], from_prev.at[h], edge_send.at[h, 0], edge_recv.at[h, 0], {"cz": z + 1}),
            remote(left_grads.at[h], from_next.at[h], edge_send.at[h, 1], edge_recv.at[h, 1], {"cz": z - 1}),
        )

    def columns(device, h):
        return out.at[:, pl.ds(pl.multiple_of((device * heads + h) * wide, HD), wide)]

    for h in range(heads):
        up, down = edge_copies(h)
        pl.when(z < pairs_total - 1)(up.start)
        pl.when(z > 0)(down.start)
    sends, locals_ = [], []
    for h in range(heads):
        up, down = edge_copies(h)
        pl.when(z > 0)(up.wait_recv)
        pl.when(z < pairs_total - 1)(down.wait_recv)
        for t in range(PAIR):
            total = own_grads[h, rows(t), :]
            if t < TILES:
                near, far, table, base = from_prev, from_next, 0, t
                near_at, far_at = t, 0
            else:
                near, far, table, base = from_next, from_prev, 1, t - TILES
                near_at, far_at = NAMED + t - TILES, TILES
            total += near[h, rows(near_at), :].astype(F32)
            for s in range(NAMED):
                term = far[h, rows(far_at + s), :].astype(F32)
                total += jnp.where(slots[table, s] == base, term, 0.0)
            joined[h, rows(t), pl.ds(HD, 2 * HD)] = total.astype(BF16)
        joined[h, :, pl.ds(0, HD)] = dq[h]
        for k in range(1, ways):
            peer = (me + k) % ways
            copy = remote(joined.at[h, rows(peer)], columns(me, h), send.at[h, k], recv.at[h, k], peer_id(peer, sizes))
            copy.start()
            sends.append(copy)
        copy = pltpu.make_async_copy(joined.at[h, rows(me)], columns(me, h), local.at[h])
        copy.start()
        locals_.append(copy)
    for h in range(heads):
        for k in range(1, ways):
            source = (me + ways - k) % ways
            remote(
                joined.at[h, rows(source)], columns(source, h), send.at[h, k], recv.at[h, k], peer_id(source, sizes)
            ).wait_recv()
        locals_[h].wait()
        up, down = edge_copies(h)
        pl.when(z < pairs_total - 1)(up.wait_send)
        pl.when(z > 0)(down.wait_send)
    for copy in sends:
        copy.wait_send()


def attention_kernel(places, info, own, left, right, dq, own_grads, left_grads, right_grads, pairs, acc):
    pairs[rows(0, EDGE), :] = left[...]
    pairs[rows(EDGE, PAIR), :] = own[:, HD : 3 * HD]
    pairs[rows(EDGE + PAIR, EDGE), :] = right[...]
    acc[...] = jnp.zeros_like(acc)

    def terms_of(i):
        q = own[rows(i), :HD]
        g = own[rows(i), 3 * HD :]
        zero = jnp.zeros_like(q)
        both = jnp.concatenate(
            [jnp.concatenate([q, zero], axis=1), jnp.concatenate([zero, g], axis=1)], axis=0
        )
        where = [EDGE - 1 + i + n for n in range(3)] + [places[i, j] for j in range(LISTED)]
        live = info[0, i]
        usable = [info[1, i] > 0, None, info[2, i] > 0] + [live > j for j in range(LISTED)]
        kv = jnp.concatenate([pairs[rows(p), :] for p in where], axis=0)
        products = lax.dot_general(kv, both, (((1,), (1,)), ((), ())), preferred_element_type=F32)
        scores = []
        for n, ok in enumerate(usable):
            s = products[n * BLK : (n + 1) * BLK, :HD] * SCALE
            scores.append(s if ok is None else jnp.where(ok, s, -1e30))
        scores = jnp.concatenate(scores, axis=0)
        powers = jnp.exp(scores - jnp.max(scores, axis=0, keepdims=True))
        soft = powers * (1.0 / jnp.sum(powers, axis=0, keepdims=True))
        dp = products[:, HD:]
        ds = soft * (dp - jnp.sum(soft * dp, axis=0, keepdims=True))
        ds_low = ds.astype(BF16)
        low = jnp.concatenate([ds_low, soft.astype(BF16)], axis=1)
        terms = jnp.dot(low, both, preferred_element_type=F32)
        grad_q = lax.dot_general(ds_low, kv[:, :HD], (((0,), (0,)), ((), ())), preferred_element_type=F32)
        return where, terms, grad_q

    def step(n, carry):
        blocks = [n * TOGETHER + u for u in range(TOGETHER)]
        found = [terms_of(i) for i in blocks]
        for i, (where, terms, grad_q) in zip(blocks, found):
            dq[rows(i), :] = (grad_q * SCALE).astype(BF16)
            acc[rows(EDGE - 1 + i, 3), :] += terms[: 3 * BLK]
            for j in range(LISTED):
                acc[rows(where[3 + j]), :] += terms[(3 + j) * BLK : (4 + j) * BLK]
        return carry

    lax.fori_loop(0, PAIR // TOGETHER, step, 0)
    for k, factor in ((0, SCALE), (HD, 1.0)):
        columns = slice(k, k + HD)
        own_grads[:, columns] = acc[rows(EDGE, PAIR), columns] * factor
        left_grads[:, columns] = (acc[rows(0, EDGE), columns] * factor).astype(BF16)
        right_grads[:, columns] = (acc[rows(EDGE + PAIR, EDGE), columns] * factor).astype(BF16)


def tables(key_lists, live_counts, axes):
    pair_axis, half_axis = axes
    pairs_total = lax.axis_size(pair_axis)
    z = lax.axis_index(pair_axis)
    x = lax.axis_index(half_axis)
    mine = jnp.concatenate([key_lists, live_counts[:, None]], axis=1)
    other = lax.ppermute(mine, half_axis, [(0, 1), (1, 0)])
    pair = jnp.where(x == 0, jnp.concatenate([mine, other]), jnp.concatenate([other, mine]))
    after = lax.ppermute(pair, pair_axis, [(i + 1, i) for i in range(pairs_total - 1)])
    before = lax.ppermute(pair, pair_axis, [(i, i + 1) for i in range(pairs_total - 1)])
    base = z * PAIR
    lists = jnp.stack([after[:TILES], before[TILES:], pair[:TILES], pair[TILES:]])[:, :, :LISTED]
    lists = lists.reshape(4, TILES * LISTED)
    first = base + jnp.array([0, TILES, -PAIR, PAIR + TILES], jnp.int32)
    order = jnp.arange(TILES, dtype=jnp.int32)
    needed = jnp.any(lists[:, :, None] == (first[:, None] + order[None, :])[:, None, :], axis=1)
    earlier = order[None, :] < order[:, None]
    rank = jnp.sum(jnp.where(earlier[None] & needed[:, None, :], 1, 0), axis=2)
    slot = jnp.arange(NAMED, dtype=jnp.int32)
    chosen = needed[:, None, :] & (rank[:, None, :] == slot[None, :, None])
    slots = jnp.sum(jnp.where(chosen, order[None, None, :], 0), axis=2).astype(jnp.int32)[:2]
    rel = pair[:, :LISTED] - base
    pick = lambda table, at: jnp.sum(jnp.where(at[:, :, None] == order, table, 0), axis=2)
    far_left = pick(rank[2], rel + PAIR)
    far_right = EDGE + PAIR + TILES + pick(rank[3], rel - PAIR - TILES)
    places = jnp.where(rel < -TILES, far_left, jnp.where(rel >= PAIR + TILES, far_right, EDGE + rel))
    places = jnp.clip(places, 0, ALL - 1).astype(jnp.int32)
    block = base + jnp.arange(PAIR, dtype=jnp.int32)
    last = pairs_total * PAIR - 1
    info = jnp.stack([pair[:, LISTED], (block > 0).astype(jnp.int32), (block < last).astype(jnp.int32)])
    return slots, places, info


def shards(qkv, grad_out, key_lists, live_counts):
    heads_total = lax.axis_size("head")
    ways = lax.axis_size("cx") * heads_total
    sizes = (lax.axis_size("cz"), heads_total, ways)
    slots, places, info = tables(key_lists, live_counts, ("cz", "cx"))
    heads = qkv.shape[1] // (3 * HD) // ways
    full = qkv.shape[0] * ways
    sds = jax.ShapeDtypeStruct
    edge = sds((heads, EDGE * BLK, 2 * HD), BF16)
    vmem = pl.BlockSpec(memory_space=pltpu.VMEM)
    smem = pl.BlockSpec(memory_space=pltpu.SMEM)
    anywhere = pl.BlockSpec(memory_space=pl.ANY)
    dma = pltpu.SemaphoreType.DMA
    own, left, right = pl.pallas_call(
        functools.partial(gather_kernel, sizes),
        in_specs=[smem, anywhere, anywhere],
        out_specs=[vmem] * 3,
        out_shape=(sds((heads, full, 4 * HD), BF16), edge, edge),
        scratch_shapes=[
            pltpu.VMEM((heads, 2, NAMED * BLK, 2 * HD), BF16),
            dma((heads, ways, 2)), dma((heads, ways, 2)), dma((heads, 2)), dma((heads, 2, 2)), dma((heads, 2, 2)),
        ],
        compiler_params=pltpu.CompilerParams(collective_id=0, has_side_effects=True),
        name="gather",
    )(slots, qkv, grad_out)
    block = lambda a: pl.BlockSpec((None, *a.shape[1:]), lambda h, *_: (h, 0, 0))
    outs = (sds((heads, full, HD), BF16), sds((heads, full, 2 * HD), F32), edge, edge)
    grads = pl.pallas_call(
        attention_kernel,
        grid_spec=pltpu.PrefetchScalarGridSpec(
            num_scalar_prefetch=2,
            grid=(heads,),
            in_specs=[block(a) for a in (own, left, right)],
            out_specs=[block(a) for a in outs],
            scratch_shapes=[pltpu.VMEM((ALL * BLK, 2 * HD), BF16), pltpu.VMEM((ALL * BLK, 2 * HD), F32)],
        ),
        out_shape=outs,
        name="attention",
    )(places, info, own, left, right)
    return pl.pallas_call(
        functools.partial(return_kernel, sizes),
        in_specs=[smem, vmem, vmem, anywhere, anywhere],
        out_specs=anywhere,
        out_shape=sds(qkv.shape, BF16),
        scratch_shapes=[
            pltpu.VMEM(edge.shape, BF16), pltpu.VMEM(edge.shape, BF16), pltpu.VMEM((heads, full, 3 * HD), BF16),
            dma((heads, ways)), dma((heads, ways)), dma((heads,)), dma((heads, 2)), dma((heads, 2)),
        ],
        compiler_params=pltpu.CompilerParams(collective_id=1, has_side_effects=True),
        name="give_back",
    )(slots, *grads)


def solution(mesh):
    ctx, head = mesh.shape["ctx"], mesh.shape["head"]
    split = Mesh(mesh.devices.reshape(ctx // 2, 2, head), ("cz", "cx", "head"))
    both = ("cz", "cx")
    tokens = P((*both, "head"), None)
    return jax.shard_map(
        shards, mesh=split, in_specs=(tokens, tokens, P(both, None), P(both)), out_specs=tokens, check_vma=False
    )
```

time: 234 us -> 178 us (0.76)
  Pallas kernels: 60.4 us -> 154 us
  waiting for transfers between devices: 60.3 us -> 4.26 us
  starting transfers between devices: 49.6 us -> 8.27 us
  local copies, waits for them, and re-layouts: 35.3 us -> 5.84 us
  blocking collectives: 23.8 us -> 0 us
    pallas_call x6 -> x3, Pallas kernels: 60.4 us -> 154 us  [the longest x1 61.2 us: shards(): pl.pallas_call(functools.partial(gather_kernel, sizes), in_specs=[smem, a...]
    ppermute x8 -> x0, waiting for transfers between devices: 47.8 us -> none  [the longest x2 21.6 us: shards(): lefts.append(lax.ppermute(to_next, 'cz', up))]
    all_to_all x1 -> x0, blocking collectives: 23.8 us -> none  [shards(): lax.all_to_all(joined, group, split_axis=0, concat_axis=0, tiled=True)]
    ppermute x8 -> x0, starting transfers between devices: 22.2 us -> none  [the longest x2 10 us: shards(): from_prev = lax.ppermute(right_grads, 'cz', up)]
    all_to_all x5 -> x0, starting transfers between devices: 19.7 us -> none  [the longest x4 15.9 us: gathered(): lax.all_to_all(part.transpose(1, 0, 2), group, split_axis=0, concat_axis=...]
    reshape x3 -> x0, local copies, waits for them, and re-layouts: 12.4 us -> none  [the longest x1 7.07 us: shards(): split_qkv = qkv.reshape(tokens, ways, CHUNKS, heads * 3 * HD)]
    all_to_all x5 -> x0, waiting for transfers between devices: 8.52 us -> none  [the longest x4 8.52 us: gathered(): lax.all_to_all(part.transpose(1, 0, 2), group, split_axis=0, concat_axis=...]
    slice x2 -> x0, local copies, waits for them, and re-layouts: 8.35 us -> none  [the longest x1 6.05 us: shards(): own = gathered(split_qkv[:, :, c])]
  transfers between devices with their start and end apart: 16 -> 3, of which waited for: 10 -> 2; matrix products, arithmetic and copies ran while one was open for 12% -> 1% of each run, Pallas kernels for 26% -> 0%
where the time goes in v2:
time: 178 us; the launch traced here: 177 us
  Pallas kernels  154 us (87%)
  starting transfers between devices  8.27 us (5%)
  local copies, waits for them, and re-layouts  5.84 us (3%)
  waiting for transfers between devices  4.26 us (2%)
  other arithmetic  4.16 us (2%)
    pallas_call x1, Pallas kernels, shards(): pl.pallas_call(functools.partial(gather_kernel, sizes), in_specs=[smem, a...  61.2 us
    pallas_call x1, Pallas kernels, shards(): pl.pallas_call(functools.partial(return_kernel, sizes), in_specs=[smem, v...  53.1 us
    pallas_call x1, Pallas kernels, shards(): pl.pallas_call(attention_kernel, grid_spec=pltpu.PrefetchScalarGridSpec(n...  39.8 us
    unnamed x2, local copies, waits for them, and re-layouts  4.49 us
    ppermute x1, starting transfers between devices, tables(): lax.ppermute(pair, pair_axis, [(i, i + 1) for i in range(pairs_total - 1)])  4.01 us
  transfers between devices with their start and end apart: 3, of which 2 were waited for; matrix products, arithmetic and copies ran while one was open for 1% of the time, Pallas kernels for 0%

profile of v2, /device:TPU:0, one launch (start us, length us, event | category | flops | bytes accessed | tf_op | source)
XLA Modules:
  0.0 176.7 jit_solution(10034442325860051969)
XLA Ops:
  0.0 0.7 copy.8
  0.7 0.8 pad_add_fusion.3
  1.5 3.0 %collective-permute-start = (s32[4,5]{1,0:T(4,128)S(1)}, s32[4,5]{1,0:T(4,128)S(1)}, u32[]{:S(2)}, u32[]{:S(2)}) collective-permute-start(s32[4,5]{1,0:T(4,128)S(1)} %pad_add_fusion.3), channel_id=1, source_target_pairs={{0,4},{4,0},{1,5},{5,1},{2,6},{6,2},{3,7},{7,3},{8,12},{12,8},{9,1... | collective-permute-start | bytes 248 | tf_op jit(solution)/shard_map/ppermute | solution.py:269
  4.5 0.7 broadcast_add_fusion
  5.1 0.1 iota_add_fusion
  5.2 0.8 collective-permute-done
  6.0 0.8 add_select_fusion
  6.9 0.2 slice_reduce_fusion
  7.1 4.0 %collective-permute-start.2 = (s32[8,5]{1,0:T(8,128)S(1)}, s32[8,5]{1,0:T(8,128)S(1)}, u32[]{:S(2)}, u32[]{:S(2)}) collective-permute-start(s32[8,5]{1,0:T(8,128)S(1)} %add_select_fusion), channel_id=1, source_target_pairs={{0,8},{8,16},{16,24},{1,9},{9,17},{17,25},{2,10},{10,18},{18,26},{... | collective-permute-start | bytes 488 | tf_op jit(solution)/shard_map/ppermute | solution.py:272
  11.1 1.3 collective-permute-start.1
  12.4 0.6 pad_add_fusion.4.info
  13.0 0.1 copy.11
  13.1 0.1 copy.10
  13.1 0.0 collective-permute-done.2
  13.1 3.4 %collective-permute-done.1 = s32[8,5]{1,0:T(8,128)S(1)} collective-permute-done((s32[8,5]{1,0:T(8,128)S(1)}, s32[8,5]{1,0:T(8,128)S(1)}, u32[]{:S(2)}, u32[]{:S(2)}) %collective-permute-start.1) | collective-permute-done | bytes 192 | tf_op jit(solution)/shard_map/ppermute | solution.py:271
  16.6 0.1 eq.58
  16.7 0.2 compare_reduce_fusion
  16.9 0.2 select_reduce_fusion.2
  17.1 0.1 select_reduce_fusion.3
  17.2 0.7 copy.14.slots
  17.9 0.1 select_reduce_fusion
  18.0 0.1 copy.12
  18.1 0.1 copy.13
  18.1 0.6 select_clamp_fusion.places
  18.7 61.2 %gather.1 = (bf16[4,1024,512]{2,1,0:T(8,128)(2,1)}, bf16[4,768,256]{2,1,0:T(8,128)(2,1)}, bf16[4,768,256]{2,1,0:T(8,128)(2,1)}) custom-call(s32[2,2]{1,0:T(2,128)} %copy.14.slots, bf16[128,12288]{1,0:T(8,128)(2,1)} %qkv.1, bf16[128,4096]{1,0:T(8,128)(2,1)} %grads.1), custom_call_target="tpu_custom_call" | custom-call | tf_op jit(solution)/shard_map/gather/pallas_call | solution.py:309
  79.9 39.8 %attention.1 = (bf16[4,1024,128]{2,1,0:T(8,128)(2,1)}, f32[4,1024,256]{2,1,0:T(8,128)}, bf16[4,768,256]{2,1,0:T(8,128)(2,1)}, bf16[4,768,256]{2,1,0:T(8,128)(2,1)}) custom-call(s32[8,4]{1,0:T(8,128)} %select_clamp_fusion.places, s32[3,8]{1,0:T(4,128)} %pad_add_fusion.4.info, bf16[4,1024,512]{2,1,0:T(8,128)(2,1)} %get-tuple-element.12.own, ...), custom_call_target="tpu_custom_call" | custom-call | tf_op jit(solution)/shard_map/attention/pallas_call | solution.py:323
  119.7 53.1 %give_back.1 = bf16[128,12288]{1,0:T(8,128)(2,1)} custom-call(s32[2,2]{1,0:T(2,128)} %copy.14.slots, bf16[4,1024,128]{2,1,0:T(8,128)(2,1)} %get-tuple-element.15.dq, f32[4,1024,256]{2,1,0:T(8,128)} %get-tuple-element.16.own_grads, bf16[4,768,256]{2,1,0:T(8,128)(2,1)} %get-tuple-element.17.left_grads, bf16[4,768,256]{2,1,0:T(8,128)(2,1)} %get-tuple-element.18.right_grads), custom_call_target="tpu_custom_call" | custom-call | tf_op jit(solution)/shard_map/give_back/pallas_call | solution.py:335
  172.9 3.8 %copy.16 = bf16[128,12288]{1,0:T(8,128)(2,1)} copy(bf16[128,12288]{1,0:T(8,128)(2,1)} %give_back.1) | data formatting | bytes 6291456
  (8 shorter events, 0.0 us)
Async XLA Ops:
  1.5 4.5 %collective-permute-start = (s32[4,5]{1,0:T(4,128)S(1)}, s32[4,5]{1,0:T(4,128)S(1)}, u32[]{:S(2)}, u32[]{:S(2)}) collective-permute-start(s32[4,5]{1,0:T(4,128)S(1)} %pad_add_fusion.3), channel_id=1, source_target_pairs={{0,4},{4,0},{1,5},{5,1},{2,6},{6,2},{3,7},{7,3},{8,12},{12,8},{9,1... | collective-permute-start | bytes 248 | tf_op jit(solution)/shard_map/ppermute | solution.py:269
  7.1 6.1 %collective-permute-start.2 = (s32[8,5]{1,0:T(8,128)S(1)}, s32[8,5]{1,0:T(8,128)S(1)}, u32[]{:S(2)}, u32[]{:S(2)}) collective-permute-start(s32[8,5]{1,0:T(8,128)S(1)} %add_select_fusion), channel_id=1, source_target_pairs={{0,8},{8,16},{16,24},{1,9},{9,17},{17,25},{2,10},{10,18},{18,26},{... | collective-permute-start | bytes 488 | tf_op jit(solution)/shard_map/ppermute | solution.py:272
  11.1 5.5 %collective-permute-start.1 = (s32[8,5]{1,0:T(8,128)S(1)}, s32[8,5]{1,0:T(8,128)S(1)}, u32[]{:S(2)}, u32[]{:S(2)}) collective-permute-start(s32[8,5]{1,0:T(8,128)S(1)} %add_select_fusion), channel_id=1, source_target_pairs={{8,0},{16,8},{24,16},{9,1},{17,9},{25,17},{10,2},{18,10},{26,18},{... | collective-permute-start | bytes 488 | tf_op jit(solution)/shard_map/ppermute | solution.py:271
